TPU v7x, 256 devices: a whole 4x4x8 slice. The times are simulated.
256 devices in a mesh: rows: 32 (over y, z), cols: 8 (over x, core).
Axes of the slice: x: 4, y: 4, z: 8, core: 2. Of those that a mesh axis runs over, the one named last changes fastest.
Arguments:
- genotypes: int32 [20480, 4096], P('rows', 'cols'), may hold values from 0 to 2
- frequencies: float32 [4096], P('cols'), may hold values from 0.05 to 0.5
- traits: bfloat16 [20480, 32768], P('rows', 'cols'), may hold values from -6 to 6
- geno_sketch: bfloat16 [4096, 512], P('cols'), may hold values from -0.09375 to 0.09375
- trait_sketch: bfloat16 [32768, 512], P('cols'), may hold values from -0.03125 to 0.03125
- initial: float32 [512, 256], replicated, may hold values from -6 to 6
Outputs:
- geno_scores: bfloat16 [20480, 256], P('rows')
- trait_scores: bfloat16 [20480, 256], P('rows')
- geno_loadings: float32 [256, 4096], P('rows', 'cols')
- trait_loadings: float32 [256, 32768], P('rows', 'cols')
All inputs are finite; a program needn't handle non-finite values.
Results may differ from a plain program's by a relative error of at most 0.0059.
Values sent between devices are 32-bit elements; how exact they have to be, the bound alone decides.
A program may use at most 128 MiB of HBM per device.

v0:
```python
import math

import jax
import jax.numpy as jnp
from jax import lax
from jax.sharding import PartitionSpec as P


def standard(genotypes, frequencies):
    spread = lax.rsqrt(2.0 * frequencies * (1.0 - frequencies))
    return ((genotypes.astype(jnp.float32) - 2.0 * frequencies) * spread).astype(jnp.bfloat16)


def unit_columns(matrix):
    return matrix * lax.rsqrt(jnp.mean(matrix * matrix, axis=0, keepdims=True) + 1e-06)


def inner_product(left_side, right_side):
    return lax.dot_general(
        left_side,
        right_side,
        (((0,), (0,)), ((), ())),
        precision=lax.Precision.HIGHEST,
        preferred_element_type=jnp.float32,
    )


def on_device(genotypes, frequencies, traits, geno_sketch, trait_sketch, initial):
    people = genotypes.shape[0] * lax.axis_size("rows")
    sketch_width = geno_sketch.shape[1]
    standardized = standard(genotypes, frequencies)
    partial_geno = jnp.dot(standardized, geno_sketch, preferred_element_type=jnp.float32)
    partial_trait = jnp.dot(traits, trait_sketch, preferred_element_type=jnp.float32)
    sketch_geno, sketch_trait = lax.psum((partial_geno, partial_trait), "cols")
    gram_geno, gram_trait = lax.psum(
        (inner_product(sketch_geno, sketch_geno), inner_product(sketch_trait, sketch_trait)), "rows"
    )
    lower_geno = jnp.linalg.cholesky(gram_geno / people)
    lower_trait = jnp.linalg.cholesky(gram_trait / people)
    basis_geno = lax.linalg.triangular_solve(
        lower_geno, sketch_geno, left_side=False, lower=True, transpose_a=True
    )
    basis_trait = lax.linalg.triangular_solve(
        lower_trait, sketch_trait, left_side=False, lower=True, transpose_a=True
    )
    crossed = lax.psum(inner_product(basis_geno, basis_trait), "rows") / people
    left_dirs = unit_columns(jnp.dot(crossed, initial, precision=lax.Precision.HIGHEST))
    right_dirs = unit_columns(inner_product(crossed, left_dirs))
    root_sketch = math.sqrt(sketch_width)
    geno_scores = (
        jnp.dot(basis_geno, left_dirs, precision=lax.Precision.HIGHEST) / root_sketch
    ).astype(jnp.bfloat16)
    trait_scores = (
        jnp.dot(basis_trait, right_dirs, precision=lax.Precision.HIGHEST) / root_sketch
    ).astype(jnp.bfloat16)
    geno_width = standardized.shape[1]
    geno_term = lax.dot_general(
        geno_scores, standardized, (((0,), (0,)), ((), ())), preferred_element_type=jnp.float32
    )
    trait_term = lax.dot_general(
        trait_scores, traits, (((0,), (0,)), ((), ())), preferred_element_type=jnp.float32
    )
    summed = lax.psum_scatter(
        jnp.concatenate([geno_term, trait_term], axis=1), "rows", scatter_dimension=0, tiled=True
    )
    root_people = math.sqrt(people)
    geno_loadings = summed[:, :geno_width] / root_people
    trait_loadings = summed[:, geno_width:] / root_people
    return (geno_scores, trait_scores, geno_loadings, trait_loadings)


def solution(mesh):
    placed = (
        P("rows", "cols"),
        P("cols"),
        P("rows", "cols"),
        P("cols", None),
        P("cols", None),
        P(),
    )
    return jax.shard_map(
        on_device,
        mesh=mesh,
        in_specs=placed,
        out_specs=(P("rows", None), P("rows", None), P("rows", "cols"), P("rows", "cols")),
        check_vma=False,
    )
```

profile of v0, /device:TPU:1, one launch (start us, length us, event | category | flops | bytes accessed | tf_op | source)
XLA Modules:
  0.0 957.9 jit_solution(18372460097444687967)
XLA Ops:
  8.0 7.8 fusion.85
  15.8 1.6 fusion.48
  17.4 74.7 %all-reduce.11.cloned.1.call-done = (f32[640,512]{1,0:T(8,128)}, f32[640,512]{1,0:T(8,128)}) async-done(((f32[640,512]{1,0:T(8,128)}, f32[640,512]{1,0:T(8,128)}), (f32[640,512]{1,0:T(8,128)}, f32[640,512]{1,0:T(8,128)})) %all-reduce.11.cloned.1.call-update) | async-done | bytes 2621456 | tf_op jit(solution)/shard_map/psum | solution.py:34
  92.1 5.5 fusion.84
  97.6 3.7 fusion.86
  101.8 151.5 %all-reduce.9.cloned.1.call-done = (f32[512,512]{0,1:T(8,128)}, f32[512,512]{0,1:T(8,128)}) async-done(((f32[512,512]{0,1:T(8,128)}, f32[512,512]{0,1:T(8,128)}), (f32[512,512]{0,1:T(8,128)}, f32[512,512]{0,1:T(8,128)})) %all-reduce.9.cloned.1.call-update) | async-done | bytes 2097168 | tf_op jit(solution)/shard_map/psum | solution.py:35
  253.3 1.3 broadcast_multiply_fusion.1
  254.7 1.3 copy.11
  256.0 1.3 broadcast_multiply_fusion
  257.3 1.3 copy.13
  258.7 2.7 fusion.2
  261.4 1.0 copy-done.8
  262.3 11.7 %cholesky.358 = f32[128,128]{1,0:T(8,128)S(1)} custom-call(f32[128,128]{1,0:T(8,128)S(1)} %cholesky.439), custom_call_target="Cholesky" | custom-call | tf_op jit(solution)/shard_map/jit(cholesky)/cholesky | solution.py:39
  274.1 11.7 %cholesky.286 = f32[128,128]{1,0:T(8,128)S(1)} custom-call(f32[128,128]{1,0:T(8,128)S(1)} %cholesky.426), custom_call_target="Cholesky" | custom-call | tf_op jit(solution)/shard_map/jit(cholesky)/cholesky | solution.py:38
  286.5 10.4 %custom-call.27 = f32[1,128,128]{1,2,0:T(8,128)} custom-call(f32[1,128,128]{2,1,0:T(8,128)S(1)} %get-tuple-element.65), custom_call_target="InvertDiagBlocksLowerTriangular" | custom-call | tf_op jit(solution)/shard_map/jit(cholesky)/cholesky | solution.py:38
  297.6 10.0 %custom-call.31 = f32[1,128,128]{1,2,0:T(8,128)S(1)} custom-call(f32[1,128,128]{2,1,0:T(8,128)S(1)} %get-tuple-element.55), custom_call_target="InvertDiagBlocksLowerTriangular" | custom-call | tf_op jit(solution)/shard_map/jit(cholesky)/cholesky | solution.py:39
  307.7 1.2 constant_dynamic-update-slice_fusion.3
  308.9 1.3 convolution_subtract_fusion.6
  310.2 11.7 %cholesky.377 = f32[128,128]{1,0:T(8,128)S(1)} custom-call(f32[128,128]{1,0:T(8,128)S(1)} %cholesky.443), custom_call_target="Cholesky" | custom-call | tf_op jit(solution)/shard_map/jit(cholesky)/cholesky | solution.py:39
  322.7 9.8 %custom-call.32 = f32[1,128,128]{1,2,0:T(8,128)S(1)} custom-call(f32[1,128,128]{2,1,0:T(8,128)S(1)} %get-tuple-element.52), custom_call_target="InvertDiagBlocksLowerTriangular" | custom-call | tf_op jit(solution)/shard_map/jit(cholesky)/cholesky | solution.py:39
  332.7 1.3 convolution_subtract_fusion.8
  334.0 11.9 %cholesky.398 = f32[128,128]{1,0:T(8,128)S(1)} custom-call(f32[128,128]{1,0:T(8,128)S(1)} %cholesky.448), custom_call_target="Cholesky" | custom-call | tf_op jit(solution)/shard_map/jit(cholesky)/cholesky | solution.py:39
  346.7 9.8 %custom-call.33 = f32[1,128,128]{1,2,0:T(8,128)S(1)} custom-call(f32[1,128,128]{2,1,0:T(8,128)S(1)} %get-tuple-element.49), custom_call_target="InvertDiagBlocksLowerTriangular" | custom-call | tf_op jit(solution)/shard_map/jit(cholesky)/cholesky | solution.py:39
  356.7 1.2 convolution_subtract_fusion.10
  358.0 11.7 %cholesky.415 = f32[128,128]{1,0:T(8,128)S(1)} custom-call(f32[128,128]{1,0:T(8,128)S(1)} %convolution_subtract_fusion.10), custom_call_target="Cholesky" | custom-call | tf_op jit(solution)/shard_map/jit(cholesky)/cholesky | solution.py:39
  372.8 1.1 select_select_fusion
  374.0 11.7 %while.5 = (s32[]{:T(128)}, f32[512,512]{1,0:T(8,128)}, s32[4,2]{0,1:T(2,128)S(1)}, f32[4,128,128]{2,1,0:T(8,128)S(1)}, s32[]{:T(128)}) while((s32[]{:T(128)}, f32[512,512]{1,0:T(8,128)}, s32[4,2]{0,1:T(2,128)S(1)}, f32[4,128,128]{2,1,0:T(8,128)S(1)}, s32[]{:T(128)}) %tuple.61), condition=%wide.while_cond.clone, body=%wide.while_body.clone.sunk | while | flops 2 | bytes 131189 | solution.py:43
  374.6 2.2 bitcast_dynamic-update-slice_fusion.5
  377.6 2.2 bitcast_dynamic-update-slice_fusion.5
  380.5 2.2 bitcast_dynamic-update-slice_fusion.5
  383.5 2.2 bitcast_dynamic-update-slice_fusion.5
  385.6 39.7 %custom-call.34 = f32[4,128,128]{1,2,0:T(8,128)S(1)} custom-call(f32[4,128,128]{2,1,0:T(8,128)S(1)} %get-tuple-element.21), custom_call_target="InvertDiagBlocksLowerTriangular" | custom-call | tf_op jit(solution)/shard_map/triangular_solve/custom-call.3 | solution.py:43
  425.9 1.5 convolution_subtract_fusion.1
  427.9 2.1 convolution_subtract_fusion
  430.5 2.8 convolution_subtract_fusion.4
  433.4 1.2 fusion.55
  436.1 11.7 %cholesky.305 = f32[128,128]{1,0:T(8,128)S(1)} custom-call(f32[128,128]{1,0:T(8,128)S(1)} %cholesky.430), custom_call_target="Cholesky" | custom-call | tf_op jit(solution)/shard_map/jit(cholesky)/cholesky | solution.py:38
  448.5 9.8 %custom-call.28 = f32[1,128,128]{1,2,0:T(8,128)S(1)} custom-call(f32[1,128,128]{2,1,0:T(8,128)S(1)} %get-tuple-element.62), custom_call_target="InvertDiagBlocksLowerTriangular" | custom-call | tf_op jit(solution)/shard_map/jit(cholesky)/cholesky | solution.py:38
  458.3 1.3 convolution_dynamic-update-slice_fusion.1
  460.0 11.7 %cholesky.326 = f32[128,128]{1,0:T(8,128)S(1)} custom-call(f32[128,128]{1,0:T(8,128)S(1)} %cholesky.435), custom_call_target="Cholesky" | custom-call | tf_op jit(solution)/shard_map/jit(cholesky)/cholesky | solution.py:38
  472.4 9.8 %custom-call.29 = f32[1,128,128]{1,2,0:T(8,128)S(1)} custom-call(f32[1,128,128]{2,1,0:T(8,128)S(1)} %get-tuple-element.59), custom_call_target="InvertDiagBlocksLowerTriangular" | custom-call | tf_op jit(solution)/shard_map/jit(cholesky)/cholesky | solution.py:38
  482.8 11.7 %cholesky.343 = f32[128,128]{1,0:T(8,128)S(1)} custom-call(f32[128,128]{1,0:T(8,128)S(1)} %convolution_subtract_fusion.11), custom_call_target="Cholesky" | custom-call | tf_op jit(solution)/shard_map/jit(cholesky)/cholesky | solution.py:38
  498.0 1.1 select_select_fusion.1
  499.1 11.6 %while.4 = (s32[]{:T(128)}, f32[512,512]{1,0:T(8,128)}, s32[4,2]{0,1:T(2,128)S(1)}, f32[4,128,128]{2,1,0:T(8,128)S(1)}, s32[]{:T(128)}) while((s32[]{:T(128)}, f32[512,512]{1,0:T(8,128)}, s32[4,2]{0,1:T(2,128)S(1)}, f32[4,128,128]{2,1,0:T(8,128)S(1)}, s32[]{:T(128)}) %tuple.74), condition=%wide.while_cond, body=%wide.while_body.sunk | while | flops 2 | bytes 131189 | solution.py:40
  499.7 2.3 bitcast_dynamic-update-slice_fusion.4
  502.6 2.3 bitcast_dynamic-update-slice_fusion.4
  505.5 2.3 bitcast_dynamic-update-slice_fusion.4
  508.4 2.2 bitcast_dynamic-update-slice_fusion.4
  510.7 39.5 %custom-call.30 = f32[4,128,128]{1,2,0:T(8,128)S(1)} custom-call(f32[4,128,128]{2,1,0:T(8,128)S(1)} %get-tuple-element.20), custom_call_target="InvertDiagBlocksLowerTriangular" | custom-call | tf_op jit(solution)/shard_map/triangular_solve/custom-call.3 | solution.py:40
  550.9 1.5 convolution_subtract_fusion.3
  552.5 1.4 fusion.63
  553.9 2.1 convolution_subtract_fusion.2
  556.5 2.8 convolution_subtract_fusion.5
  560.6 3.7 fusion.18
  564.6 145.9 %all-reduce.7.cloned.1.call-done = f32[512,512]{0,1:T(8,128)} async-done(((f32[512,512]{0,1:T(8,128)}), f32[512,512]{0,1:T(8,128)}) %all-reduce.7.cloned.1.call-update) | async-done | bytes 1048592 | tf_op jit(solution)/shard_map/psum | solution.py:46
  710.5 3.3 multiply_reduce_fusion.1
  713.9 3.4 fusion
  717.4 1.0 multiply_reduce_fusion
  719.4 2.2 fusion.1
  722.4 1.9 fusion.87
  724.3 2.5 pad_maximum_fusion
  726.8 221.2 %reduce-scatter.2.cloned.1.call-done = f32[8,4608]{1,0:T(8,128)} async-done(((f32[256,4608]{1,0:T(8,128)}), f32[8,4608]{1,0:T(8,128)}) %reduce-scatter.2.cloned.1.call-update) | async-done | bytes 147472 | tf_op jit(solution)/shard_map/reduce_scatter | solution.py:63
  948.1 1.3 slice_multiply_fusion.1
  949.4 1.6 slice_multiply_fusion
  (119 shorter events, 21.1 us)
Async XLA Ops:
  7.2 8.6 copy-start
  7.2 84.9 %all-reduce.11.cloned.1.call-start = ((), (), s32[]{:S(2)}) async-start(), calls=%async_computation.4 | async-start | bytes 5242880 | tf_op jit(solution)/shard_map/psum | solution.py:34
  8.0 7.8 copy-start.3
  17.4 235.9 %all-reduce.9.cloned.1.call-start = ((), (), s32[]{:S(2)}) async-start(), calls=%async_computation.3 | async-start | bytes 4194304 | tf_op jit(solution)/shard_map/psum | solution.py:35
  92.1 5.5 copy-start.2
  101.3 609.2 %all-reduce.7.cloned.1.call-start = ((), (), s32[]{:S(2)}) async-start(), calls=%async_computation.1 | async-start | bytes 2097152 | tf_op jit(solution)/shard_map/psum | solution.py:46
  261.4 1.0 copy-start.8
  261.4 36.2 %copy-start.6 = (f32[512,512]{1,0:T(8,128)}, f32[512,512]{1,0:T(8,128)S(1)}, u32[]{:S(2)}) copy-start(f32[512,512]{1,0:T(8,128)S(1)} %get-tuple-element.77) | copy-start | bytes 3145732
  285.8 23.1 %copy-start.18 = (f32[128,128]{1,0:T(8,128)}, f32[128,128]{1,0:T(8,128)S(1)}, u32[]{:S(2)}) copy-start(f32[128,128]{1,0:T(8,128)S(1)} %cholesky.286) | copy-start | bytes 196612
  430.5 2.8 copy-start.9
  430.5 4.1 copy-start.19
  433.4 1.4 copy-start.7
  433.4 1.4 copy-start.22
  435.4 0.7 copy-start.13
  497.9 52.3 %copy-start.1 = (f32[640,512]{1,0:T(8,128)S(1)}, f32[640,512]{1,0:T(8,128)}, u32[]{:S(2)}) copy-start(f32[640,512]{1,0:T(8,128)} %get-tuple-element.40) | copy-start | bytes 3932164
  550.2 0.7 copy-start.20
  552.5 3.5 copy-start.21
  556.5 3.4 copy-start.11
  556.5 4.1 copy-start.10
  556.5 4.1 copy-start.14
  559.8 0.7 copy-start.16
  560.6 161.8 %slice-start = ((s8[5242880]{0:T(1024)(128)(4,1)}), s8[1048576]{0:T(1024)(128)(4,1)S(1)}, s32[]{:S(2)}) async-start(s8[5242880]{0:T(1024)(128)(4,1)} %bitcast.109), calls=%async_computation.5 | async-start | bytes 2097152
  564.3 383.7 %reduce-scatter.2.cloned.1.call-start = ((), (), s32[]{:S(2)}) async-start(), calls=%async_computation.2 | async-start | bytes 4866048 | tf_op jit(solution)/shard_map/reduce_scatter | solution.py:63
  710.5 6.8 copy-start.5
  710.5 7.9 copy-start.4
  713.9 8.5 slice-start.1
  717.4 1.5 copy-start.17
  718.4 1.0 copy-start.15
  721.6 0.7 copy-start.12
Sparse Core Ops, SparseCore 0:
  17.5 74.5 all-reduce.10
  101.4 151.8 all-reduce.8
  564.4 146.0 all-reduce.6
  726.9 221.0 reduce-scatter.1
where the time goes:
time: 969 us; the launch traced here: 958 us
  waiting for transfers between devices  593 us (61%)
  other arithmetic  252 us (26%)
  matrix products  61.5 us (6%)
  local copies, waits for them, and re-layouts  29.9 us (3%)
  between operations  20 us (2%)
    reduce_scatter x1, waiting for transfers between devices, on_device(): lax.psum_scatter(jnp.concatenate([geno_term, trait_term], axis=1), 'rows'...  221 us
    psum x1, waiting for transfers between devices, on_device(): lax.psum((inner_product(sketch_geno, sketch_geno), inner_product(sketch_t...  152 us
    psum x1, waiting for transfers between devices, on_device(): crossed = lax.psum(inner_product(basis_geno, basis_trait), 'rows') / people  146 us
    another operation x15, other arithmetic, on_device(): lower_geno = jnp.linalg.cholesky(gram_geno / people)  79.7 us
    another operation x15, other arithmetic, on_device(): lower_trait = jnp.linalg.cholesky(gram_trait / people)  79.5 us
    psum x1, waiting for transfers between devices, on_device(): sketch_geno, sketch_trait = lax.psum((partial_geno, partial_trait), 'cols')  74.7 us
    another operation x2, other arithmetic, on_device(): lax.linalg.triangular_solve(lower_trait, sketch_trait, left_side=False, l...  40.8 us
    another operation x3, other arithmetic, on_device(): lax.linalg.triangular_solve(lower_geno, sketch_geno, left_side=False, low...  40.7 us
  transfers between devices with their start and end apart: 4, of which 4 were waited for; matrix products, arithmetic and copies ran while one was open for 0% of the time, Pallas kernels for 0%

commit v1 on v0

v1 whole, which is shorter than its diff:
```python
import functools
import math

import jax
import jax.numpy as jnp
from jax import lax
from jax.experimental import pallas as pl
from jax.experimental.pallas import tpu as pltpu
from jax.sharding import PartitionSpec as P

HI=lax.Precision.HIGHEST
F32=jnp.float32
def dotf(a,b,ca,cb):
    return lax.dot_general(a,b,(((ca,),(cb,)),((),())),precision=HI,preferred_element_type=F32)

def factor(d_ref):
    row=lax.broadcasted_iota(jnp.int32,(8,1),0)
    for p in range(16):
        PA=[d_ref[m,8*p:8*p+8,0:128] for m in (0,1)]
        PI=[d_ref[m,8*p:8*p+8,128:256] for m in (0,1)]
        dv=[jnp.ones((8,1),F32) for m in (0,1)]
        for j in range(8):
            for m in (0,1):
                c=PA[m][:,8*p+j:8*p+j+1]
                d=c[j:j+1,:]
                dv[m]=jnp.where(row==j,d,dv[m])
                if j<7:
                    f=jnp.where(row>j,c*(1.0/d),0.0)
                    PI[m]=PI[m]-f*PI[m][j:j+1,:]
                    PA[m]=PA[m]-f*PA[m][j:j+1,:]
        T=[];U=[];V=[]
        for m in (0,1):
            s=lax.rsqrt(dv[m])
            U.append(PA[m]*s); V.append(PI[m]*s)
            d_ref[m,8*p:8*p+8,128:256]=V[m]
        if p<15:
            for m in (0,1): T.append(U[m].T)
            for g in range(p+1,16):
                for m in (0,1):
                    X=d_ref[m,8*g:8*g+8,0:128]; Y=d_ref[m,8*g:8*g+8,128:256]
                    for j in range(8):
                        t=T[m][8*g:8*g+8,j:j+1]
                        X=X-t*U[m][j:j+1,:]; Y=Y-t*V[m][j:j+1,:]
                    d_ref[m,8*g:8*g+8,0:128]=X; d_ref[m,8*g:8*g+8,128:256]=Y

def inverse_factors(a_ref,d_ref,load,fac=factor):
    eye=(lax.broadcasted_iota(jnp.int32,(128,128),0)==lax.broadcasted_iota(jnp.int32,(128,128),1)).astype(F32)
    load()
    for m in (0,1):
        a_ref[m,:,512:1024]=jnp.zeros((512,512),F32)
        for k in range(4): a_ref[m,128*k:128*k+128,512+128*k:640+128*k]=eye
    def body(k,_):
        for kk in range(4):
            @pl.when(k==kk)
            def _():
                for m in (0,1):
                    d_ref[m,:,0:128]=a_ref[m,128*kk:128*kk+128,128*kk:128*kk+128]
                    d_ref[m,:,128:256]=eye
        fac(d_ref)
        for kk in range(4):
            @pl.when(k==kk)
            def _():
                lo=128*(kk+1)
                for m in (0,1):
                    R=dotf(d_ref[m,:,128:256],a_ref[m,128*kk:128*kk+128,lo:lo+512],1,0)
                    a_ref[m,128*kk:128*kk+128,lo:lo+512]=R
                    if kk<3:
                        n=512-lo
                        a_ref[m,lo:512,lo:lo+512]=a_ref[m,lo:512,lo:lo+512]-dotf(R[:,:n].T,R,1,0)
        return 0
    lax.fori_loop(0,4,body,0)

def unit(v):
    return v*lax.rsqrt(jnp.mean(v*v,axis=0,keepdims=True)+1e-06)

def dirs_kernel(fac,gg,gt,cr,init,wg,wt,a_ref,d_ref):
    def load():
        a_ref[0,:,0:512]=gg[...]; a_ref[1,:,0:512]=gt[...]
    inverse_factors(a_ref,d_ref,load,fac)
    Mg=lambda: a_ref[0,:,512:1024]
    Mt=lambda: a_ref[1,:,512:1024]
    q=dotf(Mt(),init[...],0,0)
    u=dotf(cr[...],q,1,0)
    left=unit(dotf(Mg(),u,1,0))
    p=dotf(Mg(),left,0,0)
    v=dotf(cr[...],p,0,0)
    right=unit(dotf(Mt(),v,1,0))
    sc=1.0/math.sqrt(512.0)
    wg[...]=p*sc
    wt[...]=dotf(Mt(),right,0,0)*sc

def dirs(gg,gt,cr,init,fac=factor):
    vm=pl.BlockSpec(memory_space=pltpu.VMEM)
    return pl.pallas_call(functools.partial(dirs_kernel,fac),out_shape=[jax.ShapeDtypeStruct((512,256),F32)]*2,
      in_specs=[vm]*4,out_specs=[vm]*2,scratch_shapes=[pltpu.VMEM((2,512,1024),F32),pltpu.VMEM((2,128,256),F32)],
      compiler_params=pltpu.CompilerParams(vmem_limit_bytes=48<<20),name="dirs")(gg,gt,cr,init)


def standard(genotypes, frequencies):
    spread = lax.rsqrt(2.0 * frequencies * (1.0 - frequencies))
    return ((genotypes.astype(jnp.float32) - 2.0 * frequencies) * spread).astype(jnp.bfloat16)


def on_device(genotypes, frequencies, traits, geno_sketch, trait_sketch, initial):
    people = genotypes.shape[0] * lax.axis_size("rows")
    standardized = standard(genotypes, frequencies)
    partial_geno = jnp.dot(standardized, geno_sketch, preferred_element_type=jnp.float32)
    partial_trait = jnp.dot(traits, trait_sketch, preferred_element_type=jnp.float32)
    sketch_geno, sketch_trait = lax.psum((partial_geno, partial_trait), "cols")
    grams = lax.psum(
        (
            dotf(sketch_geno, sketch_geno, 0, 0),
            dotf(sketch_trait, sketch_trait, 0, 0),
            dotf(sketch_geno, sketch_trait, 0, 0),
        ),
        "rows",
    )
    weights_geno, weights_trait = dirs(*[g / people for g in grams], initial)
    geno_scores = jnp.dot(sketch_geno, weights_geno, precision=HI).astype(jnp.bfloat16)
    trait_scores = jnp.dot(sketch_trait, weights_trait, precision=HI).astype(jnp.bfloat16)
    geno_width = standardized.shape[1]
    geno_term = lax.dot_general(
        geno_scores, standardized, (((0,), (0,)), ((), ())), preferred_element_type=jnp.float32
    )
    trait_term = lax.dot_general(
        trait_scores, traits, (((0,), (0,)), ((), ())), preferred_element_type=jnp.float32
    )
    summed = lax.psum_scatter(
        jnp.concatenate([geno_term, trait_term], axis=1), "rows", scatter_dimension=0, tiled=True
    )
    root_people = math.sqrt(people)
    return (geno_scores, trait_scores, summed[:, :geno_width] / root_people, summed[:, geno_width:] / root_people)


def solution(mesh):
    placed = (
        P("rows", "cols"),
        P("cols"),
        P("rows", "cols"),
        P("cols", None),
        P("cols", None),
        P(),
    )
    return jax.shard_map(
        on_device,
        mesh=mesh,
        in_specs=placed,
        out_specs=(P("rows", None), P("rows", None), P("rows", "cols"), P("rows", "cols")),
        check_vma=False,
    )
```

time: 969 us -> 581 us (0.60)
  other arithmetic: 252 us -> 7.91 us
  waiting for transfers between devices: 593 us -> 452 us
  Pallas kernels: 0 us -> 74.3 us
  matrix products: 61.5 us -> 27 us
  local copies, waits for them, and re-layouts: 29.9 us -> 1.42 us
    another operation x35 -> x0, other arithmetic: 241 us -> none  [the longest x15 79.7 us: on_device(): lower_geno = jnp.linalg.cholesky(gram_geno / people)]
    psum x2 -> x1, waiting for transfers between devices: 297 us -> 156 us  [on_device(): lax.psum((dotf(sketch_geno, sketch_geno, 0, 0), dotf(sketch_trait, sketch...]
    pallas_call x0 -> x1, Pallas kernels: none -> 74.3 us  [dirs(): pl.pallas_call(functools.partial(dirs_kernel, fac), out_shape=[jax.ShapeD...]
    another operation x26 -> x0, matrix products: 26.9 us -> none  [the longest x7 9.32 us: on_device(): lax.linalg.triangular_solve(lower_geno, sketch_geno, left_side=False, low...]
    another operation x35 -> x0, local copies, waits for them, and re-layouts: 23.4 us -> none  [the longest x12 11.6 us: on_device(): lax.linalg.triangular_solve(lower_trait, sketch_trait, left_side=False, l...]
    dot_general x7 -> x5, matrix products: 22.9 us -> 15.3 us  [the longest x3 12.9 us: dotf(): lax.dot_general(a, b, (((ca,), (cb,)), ((), ())), precision=HI, preferred...]
  transfers between devices with their start and end apart: 4 -> 3, of which waited for: 4 -> 3; matrix products, arithmetic and copies ran while one was open for 0% -> 0% of each run, Pallas kernels for 0% -> 0%
where the time goes in v1:
time: 581 us; the launch traced here: 577 us
  waiting for transfers between devices  452 us (78%)
  Pallas kernels  74.3 us (13%)
  matrix products  27 us (5%)
  between operations  13.9 us (2%)
  other arithmetic  7.91 us (1%)
    reduce_scatter x1, waiting for transfers between devices, on_device(): lax.psum_scatter(jnp.concatenate([geno_term, trait_term], axis=1), 'rows'...  221 us
    psum x1, waiting for transfers between devices, on_device(): lax.psum((dotf(sketch_geno, sketch_geno, 0, 0), dotf(sketch_trait, sketch...  156 us
    psum x1, waiting for transfers between devices, on_device(): sketch_geno, sketch_trait = lax.psum((partial_geno, partial_trait), 'cols')  74.6 us
    pallas_call x1, Pallas kernels, dirs(): pl.pallas_call(functools.partial(dirs_kernel, fac), out_shape=[jax.ShapeD...  74.3 us
    dot_general x3, matrix products, dotf(): lax.dot_general(a, b, (((ca,), (cb,)), ((), ())), precision=HI, preferred...  12.9 us
  transfers between devices with their start and end apart: 3, of which 3 were waited for; matrix products, arithmetic and copies ran while one was open for 0% of the time, Pallas kernels for 0%

profile of v1, /device:TPU:1, one launch (start us, length us, event | category | flops | bytes accessed | tf_op | source)
XLA Modules:
  0.0 576.7 jit_solution(17018328408196094997)
XLA Ops:
  7.2 0.0 copy-start
  7.2 0.0 all-reduce.7.cloned.1.call-start
  7.2 0.7 broadcast_multiply_fusion.3
  8.0 0.0 copy-start.4
  8.0 7.8 %fusion.3 = f32[640,512]{1,0:T(8,128)} fusion(bf16[640,4096]{1,0:T(8,128)(2,1)} %param.8, bf16[4096,512]{1,0:T(8,128)(2,1)} %param.10), kind=kOutput, calls=%fused_computation.14 | convolution fusion | flops 2684354560 | bytes 10747904 | tf_op jit(solution)/shard_map/dot_general | solution.py:108
  15.8 0.0 copy-done
  15.8 0.0 copy-done.4
  15.8 1.6 fusion.1
  17.4 0.0 all-reduce.7.cloned.1.call-update
  17.4 0.0 all-reduce.5.cloned.1.call-start
  17.4 74.6 %all-reduce.7.cloned.1.call-done = (f32[640,512]{1,0:T(8,128)}, f32[640,512]{1,0:T(8,128)}) async-done(((f32[640,512]{1,0:T(8,128)}, f32[640,512]{1,0:T(8,128)}), (f32[640,512]{1,0:T(8,128)}, f32[640,512]{1,0:T(8,128)})) %all-reduce.7.cloned.1.call-update) | async-done | bytes 2621456 | tf_op jit(solution)/shard_map/psum | solution.py:109
  92.1 0.0 copy-start.2
  92.1 0.0 copy-start.3
  92.1 5.5 fusion.2
  97.6 0.0 copy-done.2
  97.6 0.0 copy-done.3
  97.6 3.7 fusion.5
  101.3 3.7 fusion.4
  105.0 0.0 all-reduce.5.cloned.1.call-update
  105.0 0.2 reduce-scatter.2.cloned.1.call-start
  105.2 156.0 %all-reduce.5.cloned.1.call-done = (f32[512,512]{1,0:T(8,128)}, f32[512,512]{1,0:T(8,128)}, f32[512,512]{1,0:T(8,128)}) async-done(((f32[512,512]{1,0:T(8,128)}, f32[512,512]{1,0:T(8,128)}, f32[512,512]{1,0:T(8,128)}), (f32[512,512]{1,0:T(8,128)}, f32[512,512]{1,0:T(8,128)}, f32[512,512]{1,0:T(8,128)})) %all-reduce.5.cloned.1.call-update) | async-done | bytes 3145744 | tf_op jit(solution)/shard_map/psum | solution.py:110
  261.3 0.0 copy-start.8
  261.3 0.0 copy-start.9
  261.3 1.5 broadcast_multiply_fusion.2.gg
  262.8 0.0 copy-done.8
  262.8 0.3 copy-done.9
  263.1 0.0 copy-start.1
  263.1 0.0 slice-start
  263.1 0.2 broadcast_multiply_fusion
  263.4 0.8 copy-done.1
  264.2 0.0 slice-start.1
  264.2 74.3 %dirs.1 = (f32[512,256]{1,0:T(8,128)S(1)}, f32[512,256]{1,0:T(8,128)S(1)}) custom-call(f32[512,512]{1,0:T(8,128)S(1)} %broadcast_multiply_fusion.2.gg, f32[512,512]{1,0:T(8,128)S(1)} %get-tuple-element.16.gt, f32[512,512]{1,0:T(8,128)S(1)} %get-tuple-element.15.cr, f32[512,256]{1,0:T(8,128)S(1)} %copy-done.1), custom_call_target="tpu_custom_call" | custom-call | tf_op jit(solution)/shard_map/dirs/pallas_call | solution.py:94
  338.4 1.2 convolution_convert_fusion
  339.6 0.0 copy-start.6
  339.7 0.0 copy-start.5
  339.7 1.2 convolution_convert_fusion.1
  340.9 0.2 copy-done.5
  341.1 0.0 copy-start.7
  341.1 0.4 fusion
  341.5 0.0 copy-done.6
  341.5 0.0 slice-done
  341.5 0.0 slice-done.1
  341.6 1.9 fusion.6
  343.4 0.0 copy-done.7
  343.5 2.5 pad_maximum_fusion
  346.0 0.0 reduce-scatter.2.cloned.1.call-update
  346.0 221.3 %reduce-scatter.2.cloned.1.call-done = f32[8,4608]{1,0:T(8,128)} async-done(((f32[256,4608]{1,0:T(8,128)}), f32[8,4608]{1,0:T(8,128)}) %reduce-scatter.2.cloned.1.call-update) | async-done | bytes 147472 | tf_op jit(solution)/shard_map/reduce_scatter | solution.py:128
  567.3 1.3 slice_multiply_fusion.1
  568.6 1.6 slice_multiply_fusion
  (1 shorter events, 0.0 us)
Async XLA Ops:
  7.2 8.6 %copy-start = (bf16[512,512]{1,0:T(8,128)(2,1)S(1)}, bf16[512,512]{1,0:T(8,128)(2,1)}, u32[]{:S(2)}) copy-start(bf16[512,512]{1,0:T(8,128)(2,1)} %param.9) | copy-start | bytes 1572868
  7.2 84.9 %all-reduce.7.cloned.1.call-start = ((), (), s32[]{:S(2)}) async-start(), calls=%async_computation.3 | async-start | bytes 5242880 | tf_op jit(solution)/shard_map/psum | solution.py:109
  8.0 7.8 %copy-start.4 = (s32[640,512]{1,0:T(8,128)S(1)}, s32[640,512]{1,0:T(8,128)}, u32[]{:S(2)}) copy-start(s32[640,512]{1,0:T(8,128)} %param.6) | copy-start | bytes 3932164
  17.4 243.9 %all-reduce.5.cloned.1.call-start = ((), (), s32[]{:S(2)}) async-start(), calls=%async_computation.2 | async-start | bytes 6291456 | tf_op jit(solution)/shard_map/psum | solution.py:110
  92.1 5.5 copy-start.2
  92.1 5.5 copy-start.3
  105.0 462.3 %reduce-scatter.2.cloned.1.call-start = ((), (), s32[]{:S(2)}) async-start(), calls=%async_computation.1 | async-start | bytes 4866048 | tf_op jit(solution)/shard_map/reduce_scatter | solution.py:128
  261.3 1.5 copy-start.8
  261.3 1.9 copy-start.9
  263.1 1.0 copy-start.1
  263.1 78.4 %slice-start = ((s8[5242880]{0:T(1024)(128)(4,1)}), s8[4194304]{0:T(1024)(128)(4,1)S(1)}, s32[]{:S(2)}) async-start(s8[5242880]{0:T(1024)(128)(4,1)} %bitcast.16), calls=%async_computation.4 | async-start | bytes 8388608
  264.2 77.4 %slice-start.1 = ((s8[5242880]{0:T(1024)(128)(4,1)}), s8[1048576]{0:T(1024)(128)(4,1)S(1)}, s32[]{:S(2)}) async-start(s8[5242880]{0:T(1024)(128)(4,1)} %bitcast.16), calls=%async_computation.5 | async-start | bytes 2097152
  339.6 1.9 copy-start.6
  339.7 1.4 copy-start.5
  341.1 2.3 copy-start.7
Sparse Core Ops, SparseCore 0:
  17.5 74.5 all-reduce.6
  105.1 156.0 all-reduce.4
  346.1 221.1 reduce-scatter.1

commit v2 on v1

--- a/solution.py
+++ b/solution.py
@@ -96,40 +96,399 @@
       compiler_params=pltpu.CompilerParams(vmem_limit_bytes=48<<20),name="dirs")(gg,gt,cr,init)
 
 
-def standard(genotypes, frequencies):
-    spread = lax.rsqrt(2.0 * frequencies * (1.0 - frequencies))
-    return ((genotypes.astype(jnp.float32) - 2.0 * frequencies) * spread).astype(jnp.bfloat16)
+MESH = pl.DeviceIdType.MESH
+
+
+class Place:
+    def __init__(self):
+        rows, cols = lax.axis_index("rows"), lax.axis_index("cols")
+        self.x, self.core = lax.div(cols, 2), lax.rem(cols, 2)
+        self.y, self.z = lax.div(rows, 8), lax.rem(rows, 8)
+
+    def ring(self, axis):
+        return (self.z, 8) if axis == "z" else (getattr(self, axis), 4)
+
+    def other(self, axis, step):
+        here, size = self.ring(axis)
+        return lax.rem(here + step + size, size)
+
+    def device(self, axis, step):
+        at = {"x": self.x, "y": self.y, "z": self.z, "core": self.core}
+        at[axis] = 1 - self.core if axis == "core" else self.other(axis, step)
+        return (at["y"] * 8 + at["z"], at["x"] * 2 + at["core"])
+
+
+class Net:
+    def __init__(self, place, sends, recvs):
+        self.place, self.sends, self.recvs, self.count = place, sends, recvs, 0
+
+    def greet(self, axes):
+        barrier = pltpu.get_barrier_semaphore()
+        partners = [(a, s) for a in axes for s in range(1, {"core": 2, "z": 8}.get(a, 4))]
+        for axis, step in partners:
+            pl.semaphore_signal(
+                barrier, inc=1, device_id=self.place.device(axis, step), device_id_type=MESH
+            )
+        pl.semaphore_wait(barrier, len(partners))
+
+    def send(self, source, target, axis, step=1):
+        slot = self.count
+        self.count += 1
+        copy = pltpu.make_async_remote_copy(
+            src_ref=source,
+            dst_ref=target,
+            send_sem=self.sends.at[slot],
+            recv_sem=self.recvs.at[slot],
+            device_id=self.place.device(axis, step),
+            device_id_type=MESH,
+        )
+        copy.start()
+        return copy
+
+    def scatter(self, axis, part, landing):
+        size = self.place.ring(axis)[1]
+        order = sorted(range(1, size), key=lambda s: -min(s, size - s))
+        return [
+            self.send(part(self.place.other(axis, s)), landing.at[s - 1], axis, s) for s in order
+        ]
+
+    def gather(self, axis, own):
+        size = self.place.ring(axis)[1]
+        order = sorted(range(1, size), key=lambda s: -min(s, size - s))
+        return [self.send(own, own, axis, s) for s in order]
+
+
+def finish(copies):
+    for copy in copies:
+        copy.wait()
+
+
+def rows_of(index, count):
+    return pl.ds(pl.multiple_of(index * count, count), count)
+
+
+def total_of(landing):
+    total = landing[0]
+    for s in range(1, landing.shape[0]):
+        total = total + landing[s]
+    return total
+
+
+def gram_stream(net, axes, source, land1, part1, land2, part2, land3, out3, out2, out1):
+    place = net.place
+    first, second = axes
+    i1, i2, z = place.ring(first)[0], place.ring(second)[0], place.z
+    copies = net.scatter(first, lambda i: source.at[rows_of(i, 288)], land1)
+    yield
+    finish(copies)
+    part1[...] = source[rows_of(i1, 288)] + total_of(land1)
+    copies = net.scatter(second, lambda i: part1.at[rows_of(i, 72)], land2)
+    part2[72:128] = jnp.zeros((56, 128), F32)
+    yield
+    finish(copies)
+    part2[0:72] = part1[rows_of(i2, 72)] + total_of(land2)
+    copies = net.scatter("z", lambda i: part2.at[rows_of(i, 16)], land3)
+    yield
+    finish(copies)
+    out3[rows_of(z, 16)] = part2[rows_of(z, 16)] + total_of(land3)
+    copies = net.gather("z", out3.at[rows_of(z, 16)])
+    yield
+    finish(copies)
+    out2[i2] = out3[0:72]
+    copies = net.gather(second, out2.at[i2])
+    yield
+    finish(copies)
+    out1[i1] = out2[...]
+    copies = net.gather(first, out1.at[i1])
+    yield
+    finish(copies)
+
+
+GRAM_SCRATCH = [
+    pltpu.VMEM((3, 288, 128), F32),
+    pltpu.VMEM((288, 128), F32),
+    pltpu.VMEM((3, 72, 128), F32),
+    pltpu.VMEM((128, 128), F32),
+    pltpu.VMEM((7, 16, 128), F32),
+    pltpu.VMEM((128, 128), F32),
+    pltpu.VMEM((4, 72, 128), F32),
+    pltpu.VMEM((4, 4, 72, 128), F32),
+]
+UPPER = [(i, j) for j in range(4) for i in range(j + 1)]
+
+
+def together(streams):
+    streams = list(streams)
+    while streams:
+        alive = []
+        for stream in streams:
+            try:
+                next(stream)
+                alive.append(stream)
+            except StopIteration:
+                pass
+        streams = alive
+
+
+def sketch_kernel(people, geno, shift, spread, traits, gsk, tsk, gg, gt, cr, own, std, *scratch):
+    give, take, held, land, both, source, final = scratch[:7]
+    alpha, beta = scratch[7:15], scratch[15:23]
+    place = Place()
+    net = Net(place, scratch[23], scratch[24])
+    x, k = place.x, place.core
+    std[...] = ((geno[...].astype(F32) - shift[...]) * spread[...]).astype(jnp.bfloat16)
+
+    def piece(half, j):
+        rows = rows_of(half, 320)
+        if j < 2:
+            return jnp.dot(std[rows], gsk[:, 256 * j : 256 * j + 256], preferred_element_type=F32)
+        j -= 2
+        return jnp.dot(traits[rows], tsk[:, 256 * j : 256 * j + 256], preferred_element_type=F32)
+
+    net.greet(("core", "x", "y", "z"))
+    copies = []
+    for j in (2, 3, 0, 1):
+        give[j] = piece(1 - k, j)
+        copies.append(net.send(give.at[j], take.at[j], "core"))
+    for j in (2, 3, 0, 1):
+        held[j] = piece(k, j)
+    for j, copy in zip((2, 3, 0, 1), copies):
+        copy.wait()
+        held[j] = held[j] + take[j]
+    finish(net.scatter("x", lambda i: held.at[:, rows_of(i, 80)], land))
+    for j in range(4):
+        mine = held[j, rows_of(x, 80)]
+        for s in range(3):
+            mine = mine + land[s, j]
+        both[k, :, 256 * j : 256 * j + 256] = mine
+    copy = net.send(both.at[k], both.at[k], "core")
+    own[...] = both[k]
+    copy.wait()
+    flat = both[...].reshape(160, 1024)
+    view = both[:, :, pl.ds(pl.multiple_of(512 * k, 512), 512)].reshape(160, 512)
+    side = both[:, :, pl.ds(pl.multiple_of(512 + 256 * k, 256), 256)].reshape(160, 256)
+    gram = dotf(view.T, view, 1, 0)
+    for t, (i, j) in enumerate(UPPER):
+        source[128 * t : 128 * t + 128] = gram[128 * i : 128 * i + 128, 128 * j : 128 * j + 128]
+    cross = dotf(flat[:, 0:512].T, side, 1, 0)
+    for j in range(2):
+        for i in range(4):
+            t = 10 + 4 * j + i
+            source[128 * t : 128 * t + 128] = cross[128 * i : 128 * i + 128, 128 * j : 128 * j + 128]
+    together(
+        [
+            gram_stream(net, ("x", "y"), source.at[0:1152], *alpha),
+            gram_stream(net, ("y", "x"), source.at[1152:2304], *beta),
+        ]
+    )
+    for s, stream in enumerate((alpha, beta)):
+        for i in range(4):
+            for j in range(4):
+                at = 1152 * s + 288 * i + 72 * j
+                final[k, at : at + 72] = stream[7][i, j]
+    net.send(final.at[k], final.at[k], "core").wait()
+    scale = 1.0 / people
+    for v, gram_out in enumerate((gg, gt)):
+        gram_out[...] = jnp.zeros((512, 512), F32)
+        for t, (i, j) in enumerate(UPPER):
+            gram_out[128 * i : 128 * i + 128, 128 * j : 128 * j + 128] = (
+                final[v, 128 * t : 128 * t + 128] * scale
+            )
+        for j in range(2):
+            for i in range(4):
+                t, at = 10 + 4 * j + i, 256 * v + 128 * j
+                cr[128 * i : 128 * i + 128, at : at + 128] = final[v, 128 * t : 128 * t + 128] * scale
+
+
+def sketches(people, geno, shift, spread, traits, gsk, tsk):
+    vm = pl.BlockSpec(memory_space=pltpu.VMEM)
+    square = jax.ShapeDtypeStruct((512, 512), F32)
+    sems = 4 + 3 + 1 + 2 * (2 * (3 + 3 + 7)) + 1
+    return pl.pallas_call(
+        functools.partial(sketch_kernel, people),
+        out_shape=[
+            square,
+            square,
+            square,
+            jax.ShapeDtypeStruct((80, 1024), F32),
+            jax.ShapeDtypeStruct((640, 512), jnp.bfloat16),
+        ],
+        in_specs=[vm] * 6,
+        out_specs=[vm] * 5,
+        scratch_shapes=[
+            pltpu.VMEM((4, 320, 256), F32),
+            pltpu.VMEM((4, 320, 256), F32),
+            pltpu.VMEM((4, 320, 256), F32),
+            pltpu.VMEM((3, 4, 80, 256), F32),
+            pltpu.VMEM((2, 80, 1024), F32),
+            pltpu.VMEM((2304, 128), F32),
+            pltpu.VMEM((2, 2304, 128), F32),
+            *GRAM_SCRATCH,
+            *GRAM_SCRATCH,
+            pltpu.SemaphoreType.DMA((sems,)),
+            pltpu.SemaphoreType.DMA((sems,)),
+        ],
+        compiler_params=pltpu.CompilerParams(
+            collective_id=1, has_side_effects=True, vmem_limit_bytes=56 << 20
+        ),
+        name="sketches",
+    )(geno, shift, spread, traits, gsk, tsk)
+
+
+def rows_first(net, source, land1, part1, land2, out):
+    place = net.place
+    copies = net.scatter("y", lambda i: source.at[i], land1)
+    yield
+    finish(copies)
+    part1[...] = source[place.y] + total_of(land1)
+    copies = net.scatter("z", lambda i: part1.at[i], land2)
+    yield
+    finish(copies)
+    out[...] = part1[place.z] + total_of(land2)
+
+
+def ring_first(net, source, lands, part1, land2, out):
+    place = net.place
+    half = source.shape[-1] // 2
+    spans = (slice(0, half), slice(half, 2 * half))
+    arriving = {}
+    for d, step in enumerate((1, 7)):
+        far = place.other("z", 4)
+        arriving[d] = [
+            net.send(source.at[:, far, :, spans[d]], lands.at[d, 0, :, :, spans[d]], "z", step)
+        ]
+    yield
+    sent = []
+    for hop in (1, 2, 3):
+        leaving = {0: [], 1: []}
+        for part in (0, 1):
+            for d, step in enumerate((1, 7)):
+                turn = 4 - hop if d == 0 else 4 + hop
+                chunk = place.other("z", turn)
+                passed = lands.at[d, hop - 1]
+                if hop == 1:
+                    if part == 0:
+                        arriving[d][0].wait_recv()
+                        sent.append(arriving[d][0])
+                        passed[:, :, spans[d]] = passed[:, :, spans[d]] + source[:, chunk, :, spans[d]]
+                        origin = passed.at[:, :, spans[d]]
+                        which = d
+                    else:
+                        origin = source.at[:, chunk, :, spans[1 - d]]
+                        which = 1 - d
+                else:
+                    which = d if part == 0 else 1 - d
+                    arriving[d][part].wait_recv()
+                    sent.append(arriving[d][part])
+                    passed[:, :, spans[which]] = (
+                        passed[:, :, spans[which]] + source[:, chunk, :, spans[which]]
+                    )
+                    origin = passed.at[:, :, spans[which]]
+                leaving[d].append(
+                    net.send(origin, lands.at[d, hop, :, :, spans[which]], "z", step)
+                )
+        arriving = leaving
+        yield
+    for d in (0, 1):
+        for copy in arriving[d]:
+            copy.wait_recv()
+            sent.append(copy)
+    for copy in sent:
+        copy.wait_send()
+    part1[...] = source[:, place.z] + lands[0, 3] + lands[1, 3]
+    copies = net.scatter("y", lambda i: part1.at[i], land2)
+    yield
+    finish(copies)
+    out[...] = part1[place.y] + total_of(land2)
+
+
+def loading_kernel(people, own, wg, wt, std, traits, gsc, tsc, gl, tl, *scratch):
+    score, left, right = scratch[:3]
+    alpha, beta = scratch[3:7], scratch[7:11]
+    place = Place()
+    net = Net(place, scratch[11], scratch[12])
+    x, k = place.x, place.core
+    score[k, x, :, 0:256] = dotf(own[:, 0:512], wg[...], 1, 0).astype(jnp.bfloat16).astype(F32)
+    score[k, x, :, 256:512] = dotf(own[:, 512:1024], wt[...], 1, 0).astype(jnp.bfloat16).astype(F32)
+    net.greet(("core", "x", "y", "z"))
+    mine = score.at[k, x]
+    across = [net.send(mine, mine, "x", s) for s in (2, 1, 3)]
+    pair = [net.send(mine, mine, "core")]
+    for s, copy in zip((2, 1, 3), across):
+        copy.wait()
+        came = score.at[k, place.other("x", -s)]
+        pair.append(net.send(came, came, "core"))
+    finish(pair)
+    full = score[...].reshape(640, 512).astype(jnp.bfloat16)
+    gsc[...] = full[:, 0:256]
+    tsc[...] = full[:, 256:512]
+    geno_t, trait_t = full[:, 0:256].T, full[:, 256:512].T
+
+    def put(target, at, lhs, rhs):
+        width = rhs.shape[1]
+        target[:, :, :, at : at + width] = jnp.dot(lhs, rhs, preferred_element_type=F32).reshape(
+            4, 8, 8, width
+        )
+
+    for at in range(0, 1792, 256):
+        put(right, at, trait_t, traits[:, 2304 + at : 2560 + at])
+    for at in range(0, 512, 256):
+        put(right, 1792 + at, geno_t, std[:, at : at + 256])
+    second = ring_first(net, right, *beta)
+    next(second)
+    for at in range(0, 2304, 256):
+        put(left, at, trait_t, traits[:, at : at + 256])
+    together([rows_first(net, left, *alpha), second])
+    scale = 1.0 / math.sqrt(people)
+    tl[:, 0:2304] = alpha[3][...] * scale
+    tl[:, 2304:4096] = beta[3][:, 0:1792] * scale
+    gl[...] = beta[3][:, 1792:2304] * scale
+
+
+def loadings(people, own, wg, wt, std, traits):
+    vm = pl.BlockSpec(memory_space=pltpu.VMEM)
+    sems = 3 + 4 + 10 + 14 + 3
+    return pl.pallas_call(
+        functools.partial(loading_kernel, people),
+        out_shape=[
+            jax.ShapeDtypeStruct((640, 256), jnp.bfloat16),
+            jax.ShapeDtypeStruct((640, 256), jnp.bfloat16),
+            jax.ShapeDtypeStruct((8, 512), F32),
+            jax.ShapeDtypeStruct((8, 4096), F32),
+        ],
+        in_specs=[vm] * 5,
+        out_specs=[vm] * 4,
+        scratch_shapes=[
+            pltpu.VMEM((2, 4, 80, 512), F32),
+            pltpu.VMEM((4, 8, 8, 2304), F32),
+            pltpu.VMEM((4, 8, 8, 2304), F32),
+            pltpu.VMEM((3, 8, 8, 2304), F32),
+            pltpu.VMEM((8, 8, 2304), F32),
+            pltpu.VMEM((7, 8, 2304), F32),
+            pltpu.VMEM((8, 2304), F32),
+            pltpu.VMEM((2, 4, 4, 8, 2304), F32),
+            pltpu.VMEM((4, 8, 2304), F32),
+            pltpu.VMEM((3, 8, 2304), F32),
+            pltpu.VMEM((8, 2304), F32),
+            pltpu.SemaphoreType.DMA((sems,)),
+            pltpu.SemaphoreType.DMA((sems,)),
+        ],
+        compiler_params=pltpu.CompilerParams(
+            collective_id=2, has_side_effects=True, vmem_limit_bytes=56 << 20
+        ),
+        name="loadings",
+    )(own, wg, wt, std, traits)
 
 
 def on_device(genotypes, frequencies, traits, geno_sketch, trait_sketch, initial):
     people = genotypes.shape[0] * lax.axis_size("rows")
-    standardized = standard(genotypes, frequencies)
-    partial_geno = jnp.dot(standardized, geno_sketch, preferred_element_type=jnp.float32)
-    partial_trait = jnp.dot(traits, trait_sketch, preferred_element_type=jnp.float32)
-    sketch_geno, sketch_trait = lax.psum((partial_geno, partial_trait), "cols")
-    grams = lax.psum(
-        (
-            dotf(sketch_geno, sketch_geno, 0, 0),
-            dotf(sketch_trait, sketch_trait, 0, 0),
-            dotf(sketch_geno, sketch_trait, 0, 0),
-        ),
-        "rows",
+    shift = (2.0 * frequencies)[None, :]
+    spread = lax.rsqrt(2.0 * frequencies * (1.0 - frequencies))[None, :]
+    gg, gt, cr, own, std = sketches(
+        people, genotypes, shift, spread, traits, geno_sketch, trait_sketch
     )
-    weights_geno, weights_trait = dirs(*[g / people for g in grams], initial)
-    geno_scores = jnp.dot(sketch_geno, weights_geno, precision=HI).astype(jnp.bfloat16)
-    trait_scores = jnp.dot(sketch_trait, weights_trait, precision=HI).astype(jnp.bfloat16)
-    geno_width = standardized.shape[1]
-    geno_term = lax.dot_general(
-        geno_scores, standardized, (((0,), (0,)), ((), ())), preferred_element_type=jnp.float32
-    )
-    trait_term = lax.dot_general(
-        trait_scores, traits, (((0,), (0,)), ((), ())), preferred_element_type=jnp.float32
-    )
-    summed = lax.psum_scatter(
-        jnp.concatenate([geno_term, trait_term], axis=1), "rows", scatter_dimension=0, tiled=True
-    )
-    root_people = math.sqrt(people)
-    return (geno_scores, trait_scores, summed[:, :geno_width] / root_people, summed[:, geno_width:] / root_people)
+    weights_geno, weights_trait = dirs(gg, gt, cr, initial)
+    return tuple(loadings(people, own, weights_geno, weights_trait, std, traits))
 
 
 def solution(mesh):

time: 581 us -> 252 us (0.43)
  waiting for transfers between devices: 452 us -> 0 us
  Pallas kernels: 74.3 us -> 238 us
  matrix products: 27 us -> 0 us
  between operations: 13.9 us -> 0.69 us
  local copies, waits for them, and re-layouts: 1.42 us -> 11.6 us
  other arithmetic: 7.91 us -> 1.27 us
    psum x2 -> x0, waiting for transfers between devices: 231 us -> none  [the longest x1 156 us: on_device(): lax.psum((dotf(sketch_geno, sketch_geno, 0, 0), dotf(sketch_trait, sketch...]
    reduce_scatter x1 -> x0, waiting for transfers between devices: 221 us -> none  [on_device(): lax.psum_scatter(jnp.concatenate([geno_term, trait_term], axis=1), 'rows'...]
    pallas_call x0 -> x2, Pallas kernels: none -> 163 us  [the longest x1 83.4 us: loadings(): pl.pallas_call(functools.partial(loading_kernel, people), out_shape=[jax....]
    dot_general x9 -> x0, matrix products: 27 us -> none  [the longest x3 12.9 us: dotf(): lax.dot_general(a, b, (((ca,), (cb,)), ((), ())), precision=HI, preferred...]
    unnamed x24 -> x16, local copies, waits for them, and re-layouts: 1.42 us -> 11.6 us
  transfers between devices with their start and end apart: 3 -> 0, of which waited for: 3 -> 0; matrix products, arithmetic and copies ran while one was open for 0% -> 0% of each run, Pallas kernels for 0% -> 0%
where the time goes in v2:
time: 252 us; the launch traced here: 251 us
  Pallas kernels  238 us (94%)
  local copies, waits for them, and re-layouts  11.6 us (5%)
    pallas_call x1, Pallas kernels, loadings(): pl.pallas_call(functools.partial(loading_kernel, people), out_shape=[jax....  83.4 us
    pallas_call x1, Pallas kernels, sketches(): pl.pallas_call(functools.partial(sketch_kernel, people), out_shape=[squar...  80 us
    pallas_call x1, Pallas kernels, dirs(): pl.pallas_call(functools.partial(dirs_kernel, fac), out_shape=[jax.ShapeD...  74.4 us
    unnamed x16, local copies, waits for them, and re-layouts  11.6 us

profile of v2, /device:TPU:1, one launch (start us, length us, event | category | flops | bytes accessed | tf_op | source)
XLA Modules:
  0.0 251.3 jit_solution(1116042823116102231)
XLA Ops:
  0.6 1.3 multiply_rsqrt_fusion
  1.9 0.0 copy-start.3
  1.9 80.0 %sketches.1 = (f32[512,512]{1,0:T(8,128)}, f32[512,512]{1,0:T(8,128)}, f32[512,512]{1,0:T(8,128)}, f32[80,1024]{1,0:T(8,128)}, bf16[640,512]{1,0:T(8,128)(2,1)}) custom-call(s32[640,512]{1,0:T(8,128)} %geno.1, f32[1,512]{1,0:T(1,128)} %bitcast.3, f32[1,512]{1,0:T(1,128)} %bitcast.2, bf16[640,4096]{1,0:T(8,128)(2,1)} %traits.3, bf16[512,512]{1,0:T(8,128)(2,1)} %gsk.1, ...), custom_call_target="tpu_custom_call" | custom-call | tf_op jit(solution)/shard_map/sketches/pallas_call | solution.py:307
  81.9 0.0 copy-done.3
  81.9 0.0 copy-start
  81.9 1.2 copy-done
  83.1 0.0 copy-start.1
  83.1 1.2 copy-done.1
  84.3 0.0 copy-start.2
  84.3 1.2 copy-done.2
  85.6 74.4 %dirs.1 = (f32[512,256]{1,0:T(8,128)S(1)}, f32[512,256]{1,0:T(8,128)S(1)}) custom-call(f32[512,512]{1,0:T(8,128)S(1)} %copy-done, f32[512,512]{1,0:T(8,128)S(1)} %copy-done.1, f32[512,512]{1,0:T(8,128)S(1)} %copy-done.2, f32[512,256]{1,0:T(8,128)S(1)} %copy-done.3), custom_call_target="tpu_custom_call" | custom-call | tf_op jit(solution)/shard_map/dirs/pallas_call | solution.py:94
  160.0 0.0 copy-start.4
  160.0 0.8 copy-done.4
  160.8 0.0 copy-start.5
  160.8 0.8 copy-done.5
  161.6 83.4 %loadings.1 = (bf16[640,256]{1,0:T(8,128)(2,1)}, bf16[640,256]{1,0:T(8,128)(2,1)}, f32[8,512]{1,0:T(8,128)}, f32[8,4096]{1,0:T(8,128)}) custom-call(f32[80,1024]{1,0:T(8,128)} %get-tuple-element.11.own, f32[512,256]{1,0:T(8,128)} %copy-done.4, f32[512,256]{1,0:T(8,128)} %copy-done.5, bf16[640,512]{1,0:T(8,128)(2,1)} %get-tuple-element.17.std, ...), custom_call_target="tpu_custom_call" | custom-call | tf_op jit(solution)/shard_map/loadings/pallas_call | solution.py:451
  245.0 1.7 copy.14
  246.7 1.7 copy.15
  248.4 1.3 copy.16
  249.7 1.6 copy.17
Async XLA Ops:
  1.9 80.0 %copy-start.3 = (f32[512,256]{1,0:T(8,128)S(1)}, f32[512,256]{1,0:T(8,128)}, u32[]{:S(2)}) copy-start(f32[512,256]{1,0:T(8,128)} %init.1) | copy-start | bytes 1572868
  81.9 1.2 copy-start
  83.1 1.2 copy-start.1
  84.3 1.2 copy-start.2
  160.0 0.8 copy-start.4
  160.8 0.8 copy-start.5

commit v3 on v2

v3 whole, which is shorter than its diff:
```python
import functools
import math

import jax
import jax.numpy as jnp
from jax import lax
from jax.experimental import pallas as pl
from jax.experimental.pallas import tpu as pltpu
from jax.sharding import PartitionSpec as P

HI=lax.Precision.HIGHEST
F32=jnp.float32
def dotf(a,b,ca,cb):
    return lax.dot_general(a,b,(((ca,),(cb,)),((),())),precision=HI,preferred_element_type=F32)


def factor(d_ref):
    row = lax.broadcasted_iota(jnp.int32, (8, 128), 0)
    for p in range(16):
        rows = slice(8 * p, 8 * p + 8)
        gram, inverse = d_ref[rows, 0:128], d_ref[rows, 128:256]
        cell = {}
        for j in range(8):
            column = jnp.broadcast_to(gram[:, 8 * p + j : 8 * p + j + 1], (8, 128))
            for i in range(j, 8):
                cell[i, j] = column[i : i + 1, :]
        scales = []
        for j in range(8):
            scales.append(lax.rsqrt(cell[j, j]))
            if j == 7:
                break
            inv = 1.0 / cell[j, j]
            ratio = {i: cell[i, j] * inv for i in range(j + 1, 8)}
            for b in range(j + 1, 8):
                for i in range(b, 8):
                    cell[i, b] = cell[i, b] - ratio[i] * cell[b, j]
            factors = jnp.zeros((8, 128), F32)
            for i in range(j + 1, 8):
                factors = jnp.where(row == i, jnp.broadcast_to(ratio[i], (8, 128)), factors)
            inverse = inverse - factors * inverse[j : j + 1, :]
            gram = gram - factors * gram[j : j + 1, :]
        scale = jnp.broadcast_to(scales[0], (8, 128))
        for i in range(1, 8):
            scale = jnp.where(row == i, jnp.broadcast_to(scales[i], (8, 128)), scale)
        upper, under = gram * scale, inverse * scale
        d_ref[rows, 128:256] = under
        if p < 15:
            turned = upper.T
            for g in range(p + 1, 16):
                group = slice(8 * g, 8 * g + 8)
                left, right = d_ref[group, 0:128], d_ref[group, 128:256]
                for j in range(8):
                    times = turned[group, j : j + 1]
                    left = left - times * upper[j : j + 1, :]
                    right = right - times * under[j : j + 1, :]
                d_ref[group, 0:128] = left
                d_ref[group, 128:256] = right


def inverse_kernel(gram, out, a_ref, d_ref):
    eye = (
        lax.broadcasted_iota(jnp.int32, (128, 128), 0) == lax.broadcasted_iota(jnp.int32, (128, 128), 1)
    ).astype(F32)
    a_ref[:, 0:512] = gram[...]
    a_ref[:, 512:1024] = jnp.zeros((512, 512), F32)
    for k in range(4):
        a_ref[128 * k : 128 * k + 128, 512 + 128 * k : 640 + 128 * k] = eye

    def body(k, _):
        for kk in range(4):

            @pl.when(k == kk)
            def _():
                d_ref[:, 0:128] = a_ref[128 * kk : 128 * kk + 128, 128 * kk : 128 * kk + 128]
                d_ref[:, 128:256] = eye

        factor(d_ref)
        for kk in range(4):

            @pl.when(k == kk)
            def _():
                lo = 128 * (kk + 1)
                block = slice(128 * kk, 128 * kk + 128)
                panel = dotf(d_ref[:, 128:256], a_ref[block, lo : lo + 512], 1, 0)
                a_ref[block, lo : lo + 512] = panel
                if kk < 3:
                    a_ref[lo:512, lo : lo + 512] = a_ref[lo:512, lo : lo + 512] - dotf(
                        panel[:, : 512 - lo].T, panel, 1, 0
                    )

        return 0

    lax.fori_loop(0, 4, body, 0)
    out[...] = a_ref[:, 512:1024]


def inverse_factor(gram):
    vm = pl.BlockSpec(memory_space=pltpu.VMEM)
    return pl.pallas_call(
        inverse_kernel,
        out_shape=jax.ShapeDtypeStruct((512, 512), F32),
        in_specs=[vm],
        out_specs=vm,
        scratch_shapes=[pltpu.VMEM((512, 1024), F32), pltpu.VMEM((128, 256), F32)],
        compiler_params=pltpu.CompilerParams(vmem_limit_bytes=32 << 20),
        name="inverse_factor",
    )(gram)


MESH = pl.DeviceIdType.MESH


class Place:
    def __init__(self):
        rows, cols = lax.axis_index("rows"), lax.axis_index("cols")
        self.x, self.core = lax.div(cols, 2), lax.rem(cols, 2)
        self.y, self.z = lax.div(rows, 8), lax.rem(rows, 8)

    def ring(self, axis):
        return (self.z, 8) if axis == "z" else (getattr(self, axis), 4)

    def other(self, axis, step):
        here, size = self.ring(axis)
        return lax.rem(here + step + size, size)

    def device(self, axis, step):
        at = {"x": self.x, "y": self.y, "z": self.z, "core": self.core}
        at[axis] = 1 - self.core if axis == "core" else self.other(axis, step)
        return (at["y"] * 8 + at["z"], at["x"] * 2 + at["core"])


class Net:
    def __init__(self, place, sends, recvs):
        self.place, self.sends, self.recvs, self.count = place, sends, recvs, 0

    def greet(self, axes):
        barrier = pltpu.get_barrier_semaphore()
        partners = [(a, s) for a in axes for s in range(1, {"core": 2, "z": 8}.get(a, 4))]
        for axis, step in partners:
            pl.semaphore_signal(
                barrier, inc=1, device_id=self.place.device(axis, step), device_id_type=MESH
            )
        pl.semaphore_wait(barrier, len(partners))

    def send(self, source, target, axis, step=1):
        slot = self.count
        self.count += 1
        copy = pltpu.make_async_remote_copy(
            src_ref=source,
            dst_ref=target,
            send_sem=self.sends.at[slot],
            recv_sem=self.recvs.at[slot],
            device_id=self.place.device(axis, step),
            device_id_type=MESH,
        )
        copy.start()
        return copy

    def scatter(self, axis, part, landing):
        size = self.place.ring(axis)[1]
        order = sorted(range(1, size), key=lambda s: -min(s, size - s))
        return [
            self.send(part(self.place.other(axis, s)), landing.at[s - 1], axis, s) for s in order
        ]

    def gather(self, axis, own):
        size = self.place.ring(axis)[1]
        order = sorted(range(1, size), key=lambda s: -min(s, size - s))
        return [self.send(own, own, axis, s) for s in order]


def ring_scatter(net, axis, part, lands):
    place = net.place
    size = place.ring(axis)[1]
    turns = size // 2
    ways = ((0, 1), (1, size - 1))
    flight = {d: {d: net.send(part(place.other(axis, turns), d), lands(d, 0, d), axis, s)} for d, s in ways}
    sent = [flight[d][d] for d, _ in ways]
    for hop in range(1, turns):
        leaving = {0: {}, 1: {}}
        if hop == 1:
            for d, s in ways:
                chunk = place.other(axis, turns - 1 if d == 0 else 1 - turns)
                leaving[d][1 - d] = net.send(part(chunk, 1 - d), lands(d, 1, 1 - d), axis, s)
        yield
        for first in (True, False):
            for d, s in ways:
                h = d if first else 1 - d
                if h not in flight[d]:
                    continue
                chunk = place.other(axis, turns - hop if d == 0 else hop - turns)
                flight[d][h].wait_recv()
                passed, mine = lands(d, hop - 1, h), part(chunk, h)
                passed[...] = passed[...] + mine[...]
                leaving[d][h] = net.send(passed, lands(d, hop, h), axis, s)
        flight = leaving
        sent += [flight[d][h] for d in (0, 1) for h in (0, 1)]
    yield
    for d, _ in ways:
        for h in (0, 1):
            flight[d][h].wait_recv()
    for copy in sent:
        copy.wait_send()


def finish(copies):
    for copy in copies:
        copy.wait()


def rows_of(index, count):
    return pl.ds(pl.multiple_of(index * count, count), count)


def total_of(landing):
    total = landing[0]
    for s in range(1, landing.shape[0]):
        total = total + landing[s]
    return total


def gram_stream(net, axes, source, land1, part1, land2, part2, land3, out3, out2, out1):
    place = net.place
    first, second = axes
    i1, i2, z = place.ring(first)[0], place.ring(second)[0], place.z
    copies = net.scatter(first, lambda i: source.at[rows_of(i, 288)], land1)
    yield
    finish(copies)
    part1[...] = source[rows_of(i1, 288)] + total_of(land1)
    copies = net.scatter(second, lambda i: part1.at[rows_of(i, 72)], land2)
    part2[72:128] = jnp.zeros((56, 128), F32)
    yield
    finish(copies)
    part2[0:72] = part1[rows_of(i2, 72)] + total_of(land2)
    copies = net.scatter("z", lambda i: part2.at[rows_of(i, 16)], land3)
    yield
    finish(copies)
    out3[rows_of(z, 16)] = part2[rows_of(z, 16)] + total_of(land3)
    copies = net.gather("z", out3.at[rows_of(z, 16)])
    yield
    finish(copies)
    out2[i2] = out3[0:72]
    copies = net.gather(second, out2.at[i2])
    yield
    finish(copies)
    out1[i1] = out2[...]
    copies = net.gather(first, out1.at[i1])
    yield
    finish(copies)


GRAM_SCRATCH = [
    pltpu.VMEM((3, 288, 128), F32),
    pltpu.VMEM((288, 128), F32),
    pltpu.VMEM((3, 72, 128), F32),
    pltpu.VMEM((128, 128), F32),
    pltpu.VMEM((7, 16, 128), F32),
    pltpu.VMEM((128, 128), F32),
    pltpu.VMEM((4, 72, 128), F32),
    pltpu.VMEM((4, 4, 72, 128), F32),
]
UPPER = [(i, j) for j in range(4) for i in range(j + 1)]


def together(streams):
    streams = list(streams)
    while streams:
        alive = []
        for stream in streams:
            try:
                next(stream)
                alive.append(stream)
            except StopIteration:
                pass
        streams = alive


def share_sketch(net, full, mine):
    place = net.place
    yield
    here = full.at[mine]
    across = [net.send(here, here, "x", s) for s in (2, 1, 3)]
    yield
    yield
    yield
    yield
    pair = []
    for s, copy in zip((2, 1, 3), across):
        copy.wait()
        came = full.at[place.core * 4 + place.other("x", -s)]
        pair.append(net.send(came, came, "core"))
    yield
    finish(pair)


def sketch_kernel(people, geno, shift, spread, traits, gsk, tsk, gram_out, cross_out, full, std, *scratch):
    give, take, held, lands, both, source = scratch[:6]
    alpha, beta = scratch[6:14], scratch[14:22]
    place = Place()
    net = Net(place, scratch[22], scratch[23])
    x, k = place.x, place.core
    std[...] = ((geno[...].astype(F32) - shift[...]) * spread[...]).astype(jnp.bfloat16)

    def piece(half, j):
        rows = rows_of(half, 320)
        if j < 2:
            return jnp.dot(traits[rows], tsk[:, 256 * j : 256 * j + 256], preferred_element_type=F32)
        j -= 2
        return jnp.dot(std[rows], gsk[:, 256 * j : 256 * j + 256], preferred_element_type=F32)

    net.greet(("core", "x", "y", "z"))
    copies = []
    for j in range(4):
        give[j] = piece(1 - k, j)
        copies.append(net.send(give.at[j], take.at[j], "core"))

    def part(j, step):
        return held.at[j, rows_of(place.other("x", step), 80)]

    far, near = [], []
    for j in range(4):
        mine = piece(k, j)
        copies[j].wait()
        held[j] = mine + take[j]
        toward, away = (1, 3) if j < 2 else (3, 1)
        far.append(net.send(part(j, 2), lands.at[0, j], "x", toward))
        near.append(net.send(part(j, away), lands.at[1, j], "x", away))
    passing = []
    for j in range(4):
        toward = 1 if j < 2 else 3
        far[j].wait_recv()
        lands[0, j] = lands[0, j] + part(j, toward)[...]
        passing.append(net.send(lands.at[0, j], lands.at[2, j], "x", toward))
    for j in range(4):
        near[j].wait_recv()
        passing[j].wait_recv()
        at = 512 + 256 * j if j < 2 else 256 * j - 512
        both[k, :, at : at + 256] = part(j, 0)[...] + lands[1, j] + lands[2, j]
    copy = net.send(both.at[k], both.at[k], "core")
    full[k * 4 + x] = both[k]
    for other in far + near + passing:
        other.wait_send()
    copy.wait()
    full[(1 - k) * 4 + x] = both[1 - k]
    flat = both[...].reshape(160, 1024)
    view = both[:, :, pl.ds(pl.multiple_of(512 * k, 512), 512)].reshape(160, 512)
    side = both[:, :, pl.ds(pl.multiple_of(512 + 256 * k, 256), 256)].reshape(160, 256)
    gram = dotf(view.T, view, 1, 0)
    for t, (i, j) in enumerate(UPPER):
        source[128 * t : 128 * t + 128] = gram[128 * i : 128 * i + 128, 128 * j : 128 * j + 128]
    cross = dotf(flat[:, 0:512].T, side, 1, 0)
    for j in range(2):
        for i in range(4):
            t = 10 + 4 * j + i
            source[128 * t : 128 * t + 128] = cross[128 * i : 128 * i + 128, 128 * j : 128 * j + 128]
    together(
        [
            gram_stream(net, ("x", "y"), source.at[0:1152], *alpha),
            gram_stream(net, ("y", "x"), source.at[1152:2304], *beta),
            share_sketch(net, full, k * 4 + x),
        ]
    )
    for s, stream in enumerate((alpha, beta)):
        for i in range(4):
            for j in range(4):
                at = 1152 * s + 288 * i + 72 * j
                source[at : at + 72] = stream[7][i, j]
    scale = 1.0 / people
    gram_out[...] = jnp.zeros((512, 512), F32)
    for t, (i, j) in enumerate(UPPER):
        gram_out[128 * i : 128 * i + 128, 128 * j : 128 * j + 128] = source[128 * t : 128 * t + 128] * scale
    for j in range(2):
        for i in range(4):
            t = 10 + 4 * j + i
            cross_out[128 * i : 128 * i + 128, 128 * j : 128 * j + 128] = source[128 * t : 128 * t + 128] * scale


def sketches(people, geno, shift, spread, traits, gsk, tsk):
    vm = pl.BlockSpec(memory_space=pltpu.VMEM)
    sems = 4 + 12 + 1 + 2 * (2 * (3 + 3 + 7)) + 6
    return pl.pallas_call(
        functools.partial(sketch_kernel, people),
        out_shape=[
            jax.ShapeDtypeStruct((512, 512), F32),
            jax.ShapeDtypeStruct((512, 256), F32),
            jax.ShapeDtypeStruct((8, 80, 1024), F32),
            jax.ShapeDtypeStruct((640, 512), jnp.bfloat16),
        ],
        in_specs=[vm] * 6,
        out_specs=[vm] * 4,
        scratch_shapes=[
            pltpu.VMEM((4, 320, 256), F32),
            pltpu.VMEM((4, 320, 256), F32),
            pltpu.VMEM((4, 320, 256), F32),
            pltpu.VMEM((3, 4, 80, 256), F32),
            pltpu.VMEM((2, 80, 1024), F32),
            pltpu.VMEM((2304, 128), F32),
            *GRAM_SCRATCH,
            *GRAM_SCRATCH,
            pltpu.SemaphoreType.DMA((sems,)),
            pltpu.SemaphoreType.DMA((sems,)),
        ],
        compiler_params=pltpu.CompilerParams(
            collective_id=1, has_side_effects=True, vmem_limit_bytes=56 << 20
        ),
        name="sketches",
    )(geno, shift, spread, traits, gsk, tsk)


def unit(v):
    return v * lax.rsqrt(jnp.mean(v * v, axis=0, keepdims=True) + 1e-06)


def rows_first(net, source, land1, part1, land2, out):
    place, half = net.place, source.shape[-1] // 2
    yield from ring_scatter(
        net,
        "y",
        lambda i, h: source.at[i, :, :, half * h : half * h + half],
        lambda d, hop, h: land1.at[d, hop, :, :, half * h : half * h + half],
    )
    part1[...] = source[place.y] + land1[0, 1] + land1[1, 1]
    copies = net.scatter("z", lambda i: part1.at[i], land2)
    yield
    finish(copies)
    out[...] = part1[place.z] + total_of(land2)


def ring_first(net, source, land1, part1, land2, out):
    place, half = net.place, source.shape[-1] // 2
    yield from ring_scatter(
        net,
        "z",
        lambda i, h: source.at[:, i, :, half * h : half * h + half],
        lambda d, hop, h: land1.at[d, hop, :, :, half * h : half * h + half],
    )
    part1[...] = source[:, place.z] + land1[0, 3] + land1[1, 3]
    copies = net.scatter("y", lambda i: part1.at[i], land2)
    yield
    finish(copies)
    out[...] = part1[place.y] + total_of(land2)


def rows_scratch(width):
    return [
        pltpu.VMEM((4, 8, 8, width), F32),
        pltpu.VMEM((2, 2, 8, 8, width), F32),
        pltpu.VMEM((8, 8, width), F32),
        pltpu.VMEM((7, 8, width), F32),
        pltpu.VMEM((8, width), F32),
    ]


def ring_scratch(width):
    return [
        pltpu.VMEM((4, 8, 8, width), F32),
        pltpu.VMEM((2, 4, 4, 8, width), F32),
        pltpu.VMEM((4, 8, width), F32),
        pltpu.VMEM((3, 8, width), F32),
        pltpu.VMEM((8, width), F32),
    ]


STREAMS = (
    (rows_first, rows_scratch, 0, 1024, 0),
    (ring_first, ring_scratch, 1024, 1024, 0),
    (rows_first, rows_scratch, 2048, 1280, 0),
    (ring_first, ring_scratch, 3328, 768, 512),
)


def loading_kernel(people, inv_own, cross_own, init, sketch, std, traits, gsc, tsc, gl, tl, *scratch):
    inv, cross, people_traits = scratch[:3]
    parts = [scratch[3 + 5 * s : 8 + 5 * s] for s in range(4)]
    sends, recvs, loaded = scratch[23:26]
    place = Place()
    net = Net(place, sends, recvs)
    k = place.core
    load = pltpu.make_async_copy(traits, people_traits, loaded)
    load.start()
    net.greet(("core", "x", "y", "z"))
    cols = pl.ds(pl.multiple_of(256 * k, 256), 256)
    pair = []
    for i in range(4):
        block = (slice(128 * i, 128 * i + 128), slice(0, 128 * i + 128))
        pair.append(net.send(inv_own.at[block], inv.at[(k, *block)], "core"))
    pair.append(net.send(cross_own, cross.at[:, cols], "core"))
    inv[k] = inv_own[...]
    for i in range(3):
        inv[1 - k, 128 * i : 128 * i + 128, 128 * i + 128 : 512] = jnp.zeros((128, 384 - 128 * i), F32)
    cross[:, cols] = cross_own[...]
    finish(pair)
    left = unit(dotf(inv[0], dotf(cross[...], dotf(inv[1], init[...], 0, 0), 1, 0), 1, 0))
    scale = 1.0 / math.sqrt(inv.shape[1])
    geno_weights = dotf(inv[0], left, 0, 0)
    right = unit(dotf(inv[1], dotf(cross[...], geno_weights, 0, 0), 1, 0))
    trait_weights = dotf(inv[1], right, 0, 0)
    flat = sketch[...].reshape(640, 1024)
    tscore = dotf(flat[:, 512:1024], trait_weights * scale, 1, 0).astype(jnp.bfloat16)
    tsc[...] = tscore
    gscore = dotf(flat[:, 0:512], geno_weights * scale, 1, 0).astype(jnp.bfloat16)
    gsc[...] = gscore
    geno_t, trait_t = gscore.T, tscore.T

    def put(target, at, lhs, rhs):
        width = rhs.shape[1]
        target[:, :, :, at : at + width] = jnp.dot(lhs, rhs, preferred_element_type=F32).reshape(
            4, 8, 8, width
        )

    load.wait()
    running = []
    for (make, _, first, count, genos), part in zip(STREAMS, parts):
        for at in range(0, count, 256):
            put(part[0], at, trait_t, people_traits[:, first + at : first + at + 256])
        for at in range(0, genos, 256):
            put(part[0], count + at, geno_t, std[:, at : at + 256])
        running.append(make(net, *part))
        next(running[-1])
    together(running)
    scale = 1.0 / math.sqrt(people)
    for (_, _, first, count, genos), part in zip(STREAMS, parts):
        tl[:, first : first + count] = part[4][:, 0:count] * scale
        if genos:
            gl[...] = part[4][:, count : count + genos] * scale


def loadings(people, inv_own, cross_own, init, sketch, std, traits):
    vm = pl.BlockSpec(memory_space=pltpu.VMEM)
    sems = 5 + 2 * (6 + 7) + 2 * (14 + 3)
    return pl.pallas_call(
        functools.partial(loading_kernel, people),
        out_shape=[
            jax.ShapeDtypeStruct((640, 256), jnp.bfloat16),
            jax.ShapeDtypeStruct((640, 256), jnp.bfloat16),
            jax.ShapeDtypeStruct((8, 512), F32),
            jax.ShapeDtypeStruct((8, 4096), F32),
        ],
        in_specs=[vm] * 5 + [pl.BlockSpec(memory_space=pl.ANY)],
        out_specs=[vm] * 4,
        scratch_shapes=[
            pltpu.VMEM((2, 512, 512), F32),
            pltpu.VMEM((512, 512), F32),
            pltpu.VMEM((640, 4096), jnp.bfloat16),
            *[buffer for _, scratch, _, count, genos in STREAMS for buffer in scratch(count + genos)],
            pltpu.SemaphoreType.DMA((sems,)),
            pltpu.SemaphoreType.DMA((sems,)),
            pltpu.SemaphoreType.DMA,
        ],
        compiler_params=pltpu.CompilerParams(
            collective_id=2, has_side_effects=True, vmem_limit_bytes=56 << 20
        ),
        name="loadings",
    )(inv_own, cross_own, init, sketch, std, traits)


def on_device(genotypes, frequencies, traits, geno_sketch, trait_sketch, initial):
    people = genotypes.shape[0] * lax.axis_size("rows")
    shift = (2.0 * frequencies)[None, :]
    spread = lax.rsqrt(2.0 * frequencies * (1.0 - frequencies))[None, :]
    gram, cross, sketch, std = sketches(
        people, genotypes, shift, spread, traits, geno_sketch, trait_sketch
    )
    return tuple(loadings(people, inverse_factor(gram), cross, initial, sketch, std, traits))


def solution(mesh):
    placed = (
        P("rows", "cols"),
        P("cols"),
        P("rows", "cols"),
        P("cols", None),
        P("cols", None),
        P(),
    )
    return jax.shard_map(
        on_device,
        mesh=mesh,
        in_specs=placed,
        out_specs=(P("rows", None), P("rows", None), P("rows", "cols"), P("rows", "cols")),
        check_vma=False,
    )
```

time: 252 us -> 188 us (0.75)
  Pallas kernels: 238 us -> 177 us
  local copies, waits for them, and re-layouts: 11.6 us -> 8.52 us
    pallas_call x2, Pallas kernels: 154 us -> 99.9 us  [the longest x1 75.7 us: sketches(): pl.pallas_call(functools.partial(sketch_kernel, people), out_shape=[jax.S...]
    pallas_call x1, Pallas kernels: 83.4 us -> 77.6 us  [loadings(): pl.pallas_call(functools.partial(loading_kernel, people), out_shape=[jax....]
    unnamed x16 -> x8, local copies, waits for them, and re-layouts: 11.6 us -> 8.52 us
where the time goes in v3:
time: 188 us
  Pallas kernels  177 us (94%)
  local copies, waits for them, and re-layouts  8.52 us (5%)
    pallas_call x1, Pallas kernels, loadings(): pl.pallas_call(functools.partial(loading_kernel, people), out_shape=[jax....  77.6 us
    pallas_call x1, Pallas kernels, sketches(): pl.pallas_call(functools.partial(sketch_kernel, people), out_shape=[jax.S...  75.7 us
    pallas_call x1, Pallas kernels, inverse_factor(): pl.pallas_call(inverse_kernel, out_shape=jax.ShapeDtypeStruct((512, 512),...  24.2 us
    unnamed x8, local copies, waits for them, and re-layouts  8.52 us

profile of v3, /device:TPU:1, one launch (start us, length us, event | category | flops | bytes accessed | tf_op | source)
XLA Modules:
  0.0 188.0 jit_solution(16529516712088929956)
XLA Ops:
  0.6 1.3 multiply_rsqrt_fusion
  1.9 75.7 %sketches.1 = (f32[512,512]{1,0:T(8,128)}, f32[512,256]{1,0:T(8,128)}, f32[8,80,1024]{2,1,0:T(8,128)}, bf16[640,512]{1,0:T(8,128)(2,1)}) custom-call(s32[640,512]{1,0:T(8,128)} %geno.1, f32[1,512]{1,0:T(1,128)} %bitcast.3, f32[1,512]{1,0:T(1,128)} %bitcast.2, bf16[640,4096]{1,0:T(8,128)(2,1)} %traits.3, bf16[512,512]{1,0:T(8,128)(2,1)} %gsk.1, ...), custom_call_target="tpu_custom_call" | custom-call | tf_op jit(solution)/shard_map/sketches/pallas_call | solution.py:381
  77.6 0.0 copy-start.1
  77.6 1.2 copy-done.1
  78.9 24.2 %inverse_factor.1.inv_own = f32[512,512]{1,0:T(8,128)S(1)} custom-call(f32[512,512]{1,0:T(8,128)S(1)} %copy-done.1), custom_call_target="tpu_custom_call" | custom-call | tf_op jit(solution)/shard_map/inverse_factor/pallas_call | solution.py:99
  103.0 0.0 copy-start
  103.0 1.0 copy-done
  104.0 77.6 %loadings.1 = (bf16[640,256]{1,0:T(8,128)(2,1)}, bf16[640,256]{1,0:T(8,128)(2,1)}, f32[8,512]{1,0:T(8,128)}, f32[8,4096]{1,0:T(8,128)}) custom-call(f32[512,512]{1,0:T(8,128)} %copy-done, f32[512,256]{1,0:T(8,128)} %get-tuple-element.9.cross_own, f32[512,256]{1,0:T(8,128)} %init.1, f32[8,80,1024]{2,1,0:T(8,128)} %get-tuple-element.10.sketch, ...), custom_call_target="tpu_custom_call" | custom-call | tf_op jit(solution)/shard_map/loadings/pallas_call | solution.py:531
  181.6 1.7 copy.14
  183.4 1.7 copy.15
  185.1 1.3 copy.16
  186.4 1.6 copy.17
Async XLA Ops:
  77.6 1.2 copy-start.1
  103.0 1.0 copy-start

commit v4 on v3

v4 whole, which is shorter than its diff:
```python
import functools
import math

import jax
import jax.numpy as jnp
from jax import lax
from jax.experimental import pallas as pl
from jax.experimental.pallas import tpu as pltpu
from jax.sharding import PartitionSpec as P

HI=lax.Precision.HIGHEST
F32=jnp.float32
def dotf(a,b,ca,cb):
    return lax.dot_general(a,b,(((ca,),(cb,)),((),())),precision=HI,preferred_element_type=F32)


def factor(d_ref):
    row = lax.broadcasted_iota(jnp.int32, (8, 128), 0)
    for p in range(16):
        rows = slice(8 * p, 8 * p + 8)
        gram, inverse = d_ref[rows, 0:128], d_ref[rows, 128:256]
        cell = {}
        for j in range(8):
            column = jnp.broadcast_to(gram[:, 8 * p + j : 8 * p + j + 1], (8, 128))
            for i in range(j, 8):
                cell[i, j] = column[i : i + 1, :]
        scales = []
        for j in range(8):
            scales.append(lax.rsqrt(cell[j, j]))
            if j == 7:
                break
            inv = 1.0 / cell[j, j]
            ratio = {i: cell[i, j] * inv for i in range(j + 1, 8)}
            for b in range(j + 1, 8):
                for i in range(b, 8):
                    cell[i, b] = cell[i, b] - ratio[i] * cell[b, j]
            factors = jnp.zeros((8, 128), F32)
            for i in range(j + 1, 8):
                factors = jnp.where(row == i, jnp.broadcast_to(ratio[i], (8, 128)), factors)
            inverse = inverse - factors * inverse[j : j + 1, :]
            gram = gram - factors * gram[j : j + 1, :]
        scale = jnp.broadcast_to(scales[0], (8, 128))
        for i in range(1, 8):
            scale = jnp.where(row == i, jnp.broadcast_to(scales[i], (8, 128)), scale)
        upper, under = gram * scale, inverse * scale
        d_ref[rows, 128:256] = under
        if p < 15:
            turned = upper.T
            for g in range(p + 1, 16):
                group = slice(8 * g, 8 * g + 8)
                left, right = d_ref[group, 0:128], d_ref[group, 128:256]
                for j in range(8):
                    times = turned[group, j : j + 1]
                    left = left - times * upper[j : j + 1, :]
                    right = right - times * under[j : j + 1, :]
                d_ref[group, 0:128] = left
                d_ref[group, 128:256] = right


MESH = pl.DeviceIdType.MESH


class Place:
    def __init__(self):
        rows, cols = lax.axis_index("rows"), lax.axis_index("cols")
        self.x, self.core = lax.div(cols, 2), lax.rem(cols, 2)
        self.y, self.z = lax.div(rows, 8), lax.rem(rows, 8)

    def ring(self, axis):
        return (self.z, 8) if axis == "z" else (getattr(self, axis), 4)

    def other(self, axis, step):
        here, size = self.ring(axis)
        return lax.rem(here + step + size, size)

    def device(self, axis, step):
        at = {"x": self.x, "y": self.y, "z": self.z, "core": self.core}
        at[axis] = 1 - self.core if axis == "core" else self.other(axis, step)
        return (at["y"] * 8 + at["z"], at["x"] * 2 + at["core"])


class Net:
    def __init__(self, place, sends, recvs):
        self.place, self.sends, self.recvs, self.count = place, sends, recvs, 0

    def greet(self, axes):
        barrier = pltpu.get_barrier_semaphore()
        partners = [(a, s) for a in axes for s in range(1, {"core": 2, "z": 8}.get(a, 4))]
        for axis, step in partners:
            pl.semaphore_signal(
                barrier, inc=1, device_id=self.place.device(axis, step), device_id_type=MESH
            )
        pl.semaphore_wait(barrier, len(partners))

    def send(self, source, target, axis, step=1):
        copy = self.plan(source, target, axis, step)
        copy.start()
        return copy

    def plan(self, source, target, axis, step=1):
        slot = self.count
        self.count += 1
        return pltpu.make_async_remote_copy(
            src_ref=source,
            dst_ref=target,
            send_sem=self.sends.at[slot],
            recv_sem=self.recvs.at[slot],
            device_id=self.place.device(axis, step),
            device_id_type=MESH,
        )

    def scatter(self, axis, part, landing):
        size = self.place.ring(axis)[1]
        order = sorted(range(1, size), key=lambda s: -min(s, size - s))
        return [
            self.send(part(self.place.other(axis, s)), landing.at[s - 1], axis, s) for s in order
        ]

    def gather(self, axis, own):
        size = self.place.ring(axis)[1]
        order = sorted(range(1, size), key=lambda s: -min(s, size - s))
        return [self.send(own, own, axis, s) for s in order]


def ring_scatter(net, axis, part, lands):
    place = net.place
    size = place.ring(axis)[1]
    turns = size // 2
    ways = ((0, 1), (1, size - 1))
    flight = {d: {d: net.send(part(place.other(axis, turns), d), lands(d, 0, d), axis, s)} for d, s in ways}
    sent = [flight[d][d] for d, _ in ways]
    for hop in range(1, turns):
        leaving = {0: {}, 1: {}}
        if hop == 1:
            for d, s in ways:
                chunk = place.other(axis, turns - 1 if d == 0 else 1 - turns)
                leaving[d][1 - d] = net.send(part(chunk, 1 - d), lands(d, 1, 1 - d), axis, s)
        yield
        for first in (True, False):
            for d, s in ways:
                h = d if first else 1 - d
                if h not in flight[d]:
                    continue
                chunk = place.other(axis, turns - hop if d == 0 else hop - turns)
                flight[d][h].wait_recv()
                passed, mine = lands(d, hop - 1, h), part(chunk, h)
                passed[...] = passed[...] + mine[...]
                leaving[d][h] = net.send(passed, lands(d, hop, h), axis, s)
        flight = leaving
        sent += [flight[d][h] for d in (0, 1) for h in (0, 1)]
    yield
    for d, _ in ways:
        for h in (0, 1):
            flight[d][h].wait_recv()
    for copy in sent:
        copy.wait_send()


def finish(copies):
    for copy in copies:
        copy.wait()


def rows_of(index, count):
    return pl.ds(pl.multiple_of(index * count, count), count)


def total_of(landing):
    total = landing[0]
    for s in range(1, landing.shape[0]):
        total = total + landing[s]
    return total


def gram_stream(net, axes, source, land1, part1, land2, part2, land3, out3, out2, out1):
    place = net.place
    first, second = axes
    i1, i2, z = place.ring(first)[0], place.ring(second)[0], place.z
    copies = net.scatter(first, lambda i: source.at[rows_of(i, 288)], land1)
    yield
    finish(copies)
    part1[...] = source[rows_of(i1, 288)] + total_of(land1)
    copies = net.scatter(second, lambda i: part1.at[rows_of(i, 72)], land2)
    part2[72:128] = jnp.zeros((56, 128), F32)
    yield
    finish(copies)
    part2[0:72] = part1[rows_of(i2, 72)] + total_of(land2)
    copies = net.scatter("z", lambda i: part2.at[rows_of(i, 16)], land3)
    yield
    finish(copies)
    out3[rows_of(z, 16)] = part2[rows_of(z, 16)] + total_of(land3)
    copies = net.gather("z", out3.at[rows_of(z, 16)])
    yield
    finish(copies)
    out2[i2] = out3[0:72]
    copies = net.gather(second, out2.at[i2])
    yield
    finish(copies)
    out1[i1] = out2[...]
    copies = net.gather(first, out1.at[i1])
    yield
    finish(copies)


GRAM_SCRATCH = [
    pltpu.VMEM((3, 288, 128), F32),
    pltpu.VMEM((288, 128), F32),
    pltpu.VMEM((3, 72, 128), F32),
    pltpu.VMEM((128, 128), F32),
    pltpu.VMEM((7, 16, 128), F32),
    pltpu.VMEM((128, 128), F32),
    pltpu.VMEM((4, 72, 128), F32),
    pltpu.VMEM((4, 4, 72, 128), F32),
]
UPPER = [(i, j) for j in range(4) for i in range(j + 1)]


def together(streams):
    streams = list(streams)
    while streams:
        alive = []
        for stream in streams:
            try:
                next(stream)
                alive.append(stream)
            except StopIteration:
                pass
        streams = alive


def unit(v):
    return v * lax.rsqrt(jnp.mean(v * v, axis=0, keepdims=True) + 1e-06)


def rows_first(net, source, land1, part1, land2, out):
    place, half = net.place, source.shape[-1] // 2
    yield from ring_scatter(
        net,
        "y",
        lambda i, h: source.at[i, :, :, half * h : half * h + half],
        lambda d, hop, h: land1.at[d, hop, :, :, half * h : half * h + half],
    )
    part1[...] = source[place.y] + land1[0, 1] + land1[1, 1]
    copies = net.scatter("z", lambda i: part1.at[i], land2)
    yield
    finish(copies)
    out[...] = part1[place.z] + total_of(land2)


def ring_first(net, source, land1, part1, land2, out):
    place, half = net.place, source.shape[-1] // 2
    yield from ring_scatter(
        net,
        "z",
        lambda i, h: source.at[:, i, :, half * h : half * h + half],
        lambda d, hop, h: land1.at[d, hop, :, :, half * h : half * h + half],
    )
    part1[...] = source[:, place.z] + land1[0, 3] + land1[1, 3]
    copies = net.scatter("y", lambda i: part1.at[i], land2)
    yield
    finish(copies)
    out[...] = part1[place.y] + total_of(land2)


def rows_scratch(width):
    return [
        pltpu.VMEM((4, 8, 8, width), F32),
        pltpu.VMEM((2, 2, 8, 8, width), F32),
        pltpu.VMEM((8, 8, width), F32),
        pltpu.VMEM((7, 8, width), F32),
        pltpu.VMEM((8, width), F32),
    ]


def ring_scratch(width):
    return [
        pltpu.VMEM((4, 8, 8, width), F32),
        pltpu.VMEM((2, 4, 4, 8, width), F32),
        pltpu.VMEM((4, 8, width), F32),
        pltpu.VMEM((3, 8, width), F32),
        pltpu.VMEM((8, width), F32),
    ]


STREAMS = (
    (rows_first, rows_scratch, 0, 1024, 0),
    (ring_first, ring_scratch, 1024, 1024, 0),
    (ring_first, ring_scratch, 2048, 256, 512),
    (rows_first, rows_scratch, 2304, 1024, 0),
    (rows_first, rows_scratch, 3328, 768, 0),
)
TURNS = (0, 1, 2, 1, 0, 3, 2, 1, 0, 2, 4, 3, 1, 2, 3, 0, 4, 1, 2, 3, 4, 1, 2, 3, 4)


def invert(a_ref, d_ref, done):
    eye = (
        lax.broadcasted_iota(jnp.int32, (128, 128), 0) == lax.broadcasted_iota(jnp.int32, (128, 128), 1)
    ).astype(F32)
    a_ref[:, 512:1024] = jnp.zeros((512, 512), F32)
    for k in range(4):
        a_ref[128 * k : 128 * k + 128, 512 + 128 * k : 640 + 128 * k] = eye

    def body(k, _):
        for kk in range(4):

            @pl.when(k == kk)
            def _():
                d_ref[:, 0:128] = a_ref[128 * kk : 128 * kk + 128, 128 * kk : 128 * kk + 128]
                d_ref[:, 128:256] = eye

        factor(d_ref)
        for kk in range(4):

            @pl.when(k == kk)
            def _():
                lo = 128 * (kk + 1)
                block = slice(128 * kk, 128 * kk + 128)
                panel = dotf(d_ref[:, 128:256], a_ref[block, lo : lo + 512], 1, 0)
                a_ref[block, lo : lo + 512] = panel
                done(kk)
                if kk < 3:
                    a_ref[lo:512, lo : lo + 512] = a_ref[lo:512, lo : lo + 512] - dotf(
                        panel[:, : 512 - lo].T, panel, 1, 0
                    )

        return 0

    lax.fori_loop(0, 4, body, 0)


def cca_kernel(people, geno_in, freq, traits_in, gsk_in, tsk_in, init, scores, loads, *scratch):
    geno, traits, gsk, tsk, std, give, take, held, lands, both, source = scratch[:11]
    alpha, beta = scratch[11:19], scratch[19:27]
    a_ref, d_ref, inv, cross, full = scratch[27:32]
    parts = [scratch[32 + 5 * s : 37 + 5 * s] for s in range(5)]
    sends, recvs, loaded = scratch[57:60]
    place = Place()
    net = Net(place, sends, recvs)
    x, k = place.x, place.core
    cols = pl.ds(pl.multiple_of(256 * k, 256), 256)

    def load(slot, origin, target):
        copy = pltpu.make_async_copy(origin, target, loaded.at[slot])
        copy.start()
        return copy

    def half_load(slot, half):
        rows = rows_of(half, 320)
        return load(slot, traits_in.at[rows], traits.at[rows])

    loads_of = [
        load(0, tsk_in.at[:, 0:256], tsk.at[:, 0:256]),
        half_load(1, 1 - k),
        load(2, geno_in, geno),
        load(3, tsk_in.at[:, 256:512], tsk.at[:, 256:512]),
        load(4, gsk_in, gsk),
        half_load(5, k),
    ]
    net.greet(("core", "x", "y", "z"))

    def piece(half, j):
        rows = rows_of(half, 320)
        if j < 2:
            return jnp.dot(traits[rows], tsk[:, 256 * j : 256 * j + 256], preferred_element_type=F32)
        j -= 2
        return jnp.dot(std[rows], gsk[:, 256 * j : 256 * j + 256], preferred_element_type=F32)

    copies = []
    finish(loads_of[:2])
    for j in range(4):
        if j == 1:
            loads_of[3].wait()
        if j == 2:
            finish([loads_of[2], loads_of[4]])
            spread = lax.rsqrt(2.0 * freq[...] * (1.0 - freq[...]))
            std[...] = ((geno[...].astype(F32) - 2.0 * freq[...]) * spread).astype(jnp.bfloat16)
        give[j] = piece(1 - k, j)
        copies.append(net.send(give.at[j], take.at[j], "core"))
    loads_of[5].wait()

    def part(j, step):
        return held.at[j, rows_of(place.other("x", step), 80)]

    far, near = [], []
    for j in range(4):
        mine = piece(k, j)
        copies[j].wait()
        held[j] = mine + take[j]
        toward, away = (1, 3) if j < 2 else (3, 1)
        far.append(net.send(part(j, 2), lands.at[0, j], "x", toward))
        near.append(net.send(part(j, away), lands.at[1, j], "x", away))
    passing = []
    for j in range(4):
        toward = 1 if j < 2 else 3
        far[j].wait_recv()
        lands[0, j] = lands[0, j] + part(j, toward)[...]
        passing.append(net.send(lands.at[0, j], lands.at[2, j], "x", toward))
    for j in range(4):
        near[j].wait_recv()
        passing[j].wait_recv()
        at = 512 + 256 * j if j < 2 else 256 * j - 512
        both[k, :, at : at + 256] = part(j, 0)[...] + lands[1, j] + lands[2, j]
    copy = net.send(both.at[k], both.at[k], "core")
    for other in far + near + passing:
        other.wait_send()
    copy.wait()
    flat = both[...].reshape(160, 1024)
    view = both[:, :, pl.ds(pl.multiple_of(512 * k, 512), 512)].reshape(160, 512)
    side = both[:, :, pl.ds(pl.multiple_of(512 + 256 * k, 256), 256)].reshape(160, 256)
    gram = dotf(view.T, view, 1, 0)
    for t, (i, j) in enumerate(UPPER):
        source[128 * t : 128 * t + 128] = gram[128 * i : 128 * i + 128, 128 * j : 128 * j + 128]
    crossed = dotf(flat[:, 0:512].T, side, 1, 0)
    for j in range(2):
        for i in range(4):
            t = 10 + 4 * j + i
            source[128 * t : 128 * t + 128] = crossed[128 * i : 128 * i + 128, 128 * j : 128 * j + 128]
    together(
        [
            gram_stream(net, ("x", "y"), source.at[0:1152], *alpha),
            gram_stream(net, ("y", "x"), source.at[1152:2304], *beta),
        ]
    )
    for s, stream in enumerate((alpha, beta)):
        for i in range(4):
            for j in range(4):
                at = 1152 * s + 288 * i + 72 * j
                source[at : at + 72] = stream[7][i, j]

    full[k * 4 + x] = both[k]
    full[(1 - k) * 4 + x] = both[1 - k]
    here = full.at[k * 4 + x]
    across = [net.send(here, here, "x", s) for s in (2, 1, 3)]
    scale = 1.0 / people
    a_ref[:, 0:512] = jnp.zeros((512, 512), F32)
    for t, (i, j) in enumerate(UPPER):
        a_ref[128 * i : 128 * i + 128, 128 * j : 128 * j + 128] = source[128 * t : 128 * t + 128] * scale
    for j in range(2):
        at = pl.ds(pl.multiple_of(256 * k + 128 * j, 128), 128)
        for i in range(4):
            t = 10 + 4 * j + i
            cross[128 * i : 128 * i + 128, at] = source[128 * t : 128 * t + 128] * scale
    pair = [net.send(cross.at[:, cols], cross.at[:, cols], "core")]
    swaps = []
    for i in range(4):
        block = (slice(128 * i, 128 * i + 128), slice(0, 128 * i + 128))
        swaps.append(net.plan(inv.at[(k, *block)], inv.at[(k, *block)], "core"))
        if i < 3:
            rest = slice(128 * i + 128, 512)
            for v in range(2):
                inv[v, 128 * i : 128 * i + 128, rest] = jnp.zeros((128, 384 - 128 * i), F32)

    def done(i):
        block = (slice(128 * i, 128 * i + 128), slice(0, 128 * i + 128))
        inv[(k, *block)] = a_ref[128 * i : 128 * i + 128, 512 : 640 + 128 * i]
        swaps[i].start()

    invert(a_ref, d_ref, done)
    for s, copy in zip((2, 1, 3), across):
        copy.wait()
        came = full.at[k * 4 + place.other("x", -s)]
        pair.append(net.send(came, came, "core"))
    finish(swaps)
    pair[0].wait()
    left = unit(dotf(inv[0], dotf(cross[...], dotf(inv[1], init[...], 0, 0), 1, 0), 1, 0))
    scale = 1.0 / math.sqrt(inv.shape[1])
    geno_weights = dotf(inv[0], left, 0, 0)
    right = unit(dotf(inv[1], dotf(cross[...], geno_weights, 0, 0), 1, 0))
    trait_weights = dotf(inv[1], right, 0, 0)
    finish(pair[1:])
    flat = full[...].reshape(640, 1024)
    tscore = dotf(flat[:, 512:1024], trait_weights * scale, 1, 0).astype(jnp.bfloat16)
    trait_t = tscore.T

    def put(target, at, lhs, rhs):
        width = rhs.shape[1]
        target[:, :, :, at : at + width] = jnp.dot(lhs, rhs, preferred_element_type=F32).reshape(
            4, 8, 8, width
        )

    scores[:, 256:512] = tscore
    running = {}
    geno_t = None
    for turn in TURNS:
        if turn not in running:
            make, _, first, count, genos = STREAMS[turn]
            target = parts[turn][0]
            for at in range(0, count, 256):
                put(target, at, trait_t, traits[:, first + at : first + at + 256])
            if genos:
                gscore = dotf(flat[:, 0:512], geno_weights * scale, 1, 0).astype(jnp.bfloat16)
                scores[:, 0:256] = gscore
                geno_t = gscore.T
            for at in range(0, genos, 256):
                put(target, count + at, geno_t, std[:, at : at + 256])
            running[turn] = make(net, *parts[turn])
        next(running[turn], None)
    together(running.values())
    scale = 1.0 / math.sqrt(people)
    for (_, _, first, count, genos), part_of in zip(STREAMS, parts):
        loads[:, 512 + first : 512 + first + count] = part_of[4][:, 0:count] * scale
        if genos:
            loads[:, 0:512] = part_of[4][:, count : count + genos] * scale


def cca(people, geno, freq, traits, gsk, tsk, init):
    vm, far = pl.BlockSpec(memory_space=pltpu.VMEM), pl.BlockSpec(memory_space=pl.ANY)
    sems = 4 + 12 + 1 + 2 * (2 * (3 + 3 + 7)) + 3 + 1 + 4 + 3 + 3 * (6 + 7) + 2 * (14 + 3)
    return pl.pallas_call(
        functools.partial(cca_kernel, people),
        out_shape=[
            jax.ShapeDtypeStruct((640, 512), jnp.bfloat16),
            jax.ShapeDtypeStruct((8, 4608), F32),
        ],
        in_specs=[far, vm, far, far, far, vm],
        out_specs=[vm] * 2,
        scratch_shapes=[
            pltpu.VMEM((640, 512), jnp.int32),
            pltpu.VMEM((640, 4096), jnp.bfloat16),
            pltpu.VMEM((512, 512), jnp.bfloat16),
            pltpu.VMEM((4096, 512), jnp.bfloat16),
            pltpu.VMEM((640, 512), jnp.bfloat16),
            pltpu.VMEM((4, 320, 256), F32),
            pltpu.VMEM((4, 320, 256), F32),
            pltpu.VMEM((4, 320, 256), F32),
            pltpu.VMEM((3, 4, 80, 256), F32),
            pltpu.VMEM((2, 80, 1024), F32),
            pltpu.VMEM((2304, 128), F32),
            *GRAM_SCRATCH,
            *GRAM_SCRATCH,
            pltpu.VMEM((512, 1024), F32),
            pltpu.VMEM((128, 256), F32),
            pltpu.VMEM((2, 512, 512), F32),
            pltpu.VMEM((512, 512), F32),
            pltpu.VMEM((8, 80, 1024), F32),
            *[buffer for _, scratch, _, count, genos in STREAMS for buffer in scratch(count + genos)],
            pltpu.SemaphoreType.DMA((sems,)),
            pltpu.SemaphoreType.DMA((sems,)),
            pltpu.SemaphoreType.DMA((6,)),
        ],
        compiler_params=pltpu.CompilerParams(
            collective_id=1, has_side_effects=True, vmem_limit_bytes=60 << 20
        ),
        name="cca",
    )(geno, freq, traits, gsk, tsk, init)


def on_device(genotypes, frequencies, traits, geno_sketch, trait_sketch, initial):
    people = genotypes.shape[0] * lax.axis_size("rows")
    scores, loads = cca(
        people, genotypes, frequencies[None, :], traits, geno_sketch, trait_sketch, initial
    )
    pairs, width = initial.shape[1], genotypes.shape[1]
    return (scores[:, :pairs], scores[:, pairs:], loads[:, :width], loads[:, width:])


def solution(mesh):
    placed = (
        P("rows", "cols"),
        P("cols"),
        P("rows", "cols"),
        P("cols", None),
        P("cols", None),
        P(),
    )
    return jax.shard_map(
        on_device,
        mesh=mesh,
        in_specs=placed,
        out_specs=(P("rows", None), P("rows", None), P("rows", "cols"), P("rows", "cols")),
        check_vma=False,
    )
```

time: 188 us -> 159 us (0.85)
  Pallas kernels: 177 us -> 153 us
  local copies, waits for them, and re-layouts: 8.52 us -> 4.84 us
    pallas_call x3 -> x1, Pallas kernels: 177 us -> 153 us  [cca(): pl.pallas_call(functools.partial(cca_kernel, people), out_shape=[jax.Shap...]
    unnamed x8 -> x0, local copies, waits for them, and re-layouts: 8.52 us -> none
    slice x0 -> x3, local copies, waits for them, and re-layouts: none -> 4.84 us  [the longest x1 1.95 us: on_device(): scores[:, pairs:]]
where the time goes in v4:
time: 159 us; the launch traced here: 158 us
  Pallas kernels  153 us (96%)
  local copies, waits for them, and re-layouts  4.84 us (3%)
    pallas_call x1, Pallas kernels, cca(): pl.pallas_call(functools.partial(cca_kernel, people), out_shape=[jax.Shap...  153 us

profile of v4, /device:TPU:1, one launch (start us, length us, event | category | flops | bytes accessed | tf_op | source)
XLA Modules:
  0.0 158.5 jit_solution(5482547404120463515)
XLA Ops:
  0.6 153.0 %cca.1 = (bf16[640,512]{1,0:T(8,128)(2,1)}, f32[8,4608]{1,0:T(8,128)}) custom-call(s32[640,512]{1,0:T(8,128)} %geno_in.1, f32[1,512]{1,0:T(1,128)} %bitcast.1, bf16[640,4096]{1,0:T(8,128)(2,1)} %traits_in.1, bf16[512,512]{1,0:T(8,128)(2,1)} %gsk_in.1, bf16[4096,512]{1,0:T(8,128)(2,1)} %tsk_in.1, f32[512,256]{1,0:T(8,128)} %init.1), custom_call_target="tpu_custom_call" | custom-call | tf_op jit(solution)/shard_map/cca/pallas_call | solution.py:509
  153.6 1.9 %fusion = (bf16[640,256]{1,0:T(8,128)(2,1)}, bf16[640,256]{1,0:T(8,128)(2,1)}) fusion(bf16[640,512]{1,0:T(8,128)(2,1)} %get-tuple-element.6), kind=kLoop, calls=%fused_computation | loop fusion | bytes 1310720 | tf_op jit(solution)/shard_map/slice | solution.py:554
  155.6 1.3 slice.14
  156.9 1.6 slice.15

commit v5 on v4

--- a/solution.py
+++ b/solution.py
@@ -247,6 +247,24 @@
     out[...] = part1[place.z] + total_of(land2)
 
 
+def rings_only(net, source, land1, part1, land2, out):
+    place, half = net.place, source.shape[-1] // 2
+    yield from ring_scatter(
+        net,
+        "y",
+        lambda i, h: source.at[i, :, :, half * h : half * h + half],
+        lambda d, hop, h: land1.at[d, hop, :, :, half * h : half * h + half],
+    )
+    part1[...] = source[place.y] + land1[0, 1] + land1[1, 1]
+    yield from ring_scatter(
+        net,
+        "z",
+        lambda i, h: part1.at[i, :, half * h : half * h + half],
+        lambda d, hop, h: land2.at[d, hop, :, half * h : half * h + half],
+    )
+    out[...] = part1[place.z] + land2[0, 3] + land2[1, 3]
+
+
 def ring_first(net, source, land1, part1, land2, out):
     place, half = net.place, source.shape[-1] // 2
     yield from ring_scatter(
@@ -272,6 +290,16 @@
     ]
 
 
+def rings_scratch(width):
+    return [
+        pltpu.VMEM((4, 8, 8, width), F32),
+        pltpu.VMEM((2, 2, 8, 8, width), F32),
+        pltpu.VMEM((8, 8, width), F32),
+        pltpu.VMEM((2, 4, 8, width), F32),
+        pltpu.VMEM((8, width), F32),
+    ]
+
+
 def ring_scratch(width):
     return [
         pltpu.VMEM((4, 8, 8, width), F32),
@@ -283,13 +311,12 @@
 
 
 STREAMS = (
-    (rows_first, rows_scratch, 0, 1024, 0),
-    (ring_first, ring_scratch, 1024, 1024, 0),
-    (ring_first, ring_scratch, 2048, 256, 512),
-    (rows_first, rows_scratch, 2304, 1024, 0),
-    (rows_first, rows_scratch, 3328, 768, 0),
+    (rings_only, rings_scratch, 0, 1536, 0),
+    (ring_first, ring_scratch, 1536, 1024, 0),
+    (ring_first, ring_scratch, 2560, 512, 512),
+    (rows_first, rows_scratch, 3072, 1024, 0),
 )
-TURNS = (0, 1, 2, 1, 0, 3, 2, 1, 0, 2, 4, 3, 1, 2, 3, 0, 4, 1, 2, 3, 4, 1, 2, 3, 4)
+TURNS = (0, 1, 2, 1, 0, 3, 2, 1, 2, 0, 3, 1, 2, 0, 3)
 
 
 def invert(a_ref, d_ref, done):
@@ -332,8 +359,8 @@
     geno, traits, gsk, tsk, std, give, take, held, lands, both, source = scratch[:11]
     alpha, beta = scratch[11:19], scratch[19:27]
     a_ref, d_ref, inv, cross, full = scratch[27:32]
-    parts = [scratch[32 + 5 * s : 37 + 5 * s] for s in range(5)]
-    sends, recvs, loaded = scratch[57:60]
+    parts = [scratch[32 + 5 * s : 37 + 5 * s] for s in range(4)]
+    sends, recvs, loaded = scratch[52:55]
     place = Place()
     net = Net(place, sends, recvs)
     x, k = place.x, place.core
@@ -505,7 +532,7 @@
 
 def cca(people, geno, freq, traits, gsk, tsk, init):
     vm, far = pl.BlockSpec(memory_space=pltpu.VMEM), pl.BlockSpec(memory_space=pl.ANY)
-    sems = 4 + 12 + 1 + 2 * (2 * (3 + 3 + 7)) + 3 + 1 + 4 + 3 + 3 * (6 + 7) + 2 * (14 + 3)
+    sems = 4 + 12 + 1 + 2 * (2 * (3 + 3 + 7)) + 3 + 1 + 4 + 3 + (6 + 14) + (6 + 7) + 2 * (14 + 3)
     return pl.pallas_call(
         functools.partial(cca_kernel, people),
         out_shape=[

time: 159 us -> 157 us (0.987)
  no operation moved by 1% of the time
where the time goes in v5:
time: 157 us
  Pallas kernels  152 us (97%)
  local copies, waits for them, and re-layouts  4.84 us (3%)
    pallas_call x1, Pallas kernels, cca(): pl.pallas_call(functools.partial(cca_kernel, people), out_shape=[jax.Shap...  152 us

profile of v5, /device:TPU:1, one launch (start us, length us, event | category | flops | bytes accessed | tf_op | source)
XLA Modules:
  0.0 157.0 jit_solution(15776243952969645989)
XLA Ops:
  0.6 151.5 %cca.1 = (bf16[640,512]{1,0:T(8,128)(2,1)}, f32[8,4608]{1,0:T(8,128)}) custom-call(s32[640,512]{1,0:T(8,128)} %geno_in.1, f32[1,512]{1,0:T(1,128)} %bitcast.1, bf16[640,4096]{1,0:T(8,128)(2,1)} %traits_in.1, bf16[512,512]{1,0:T(8,128)(2,1)} %gsk_in.1, bf16[4096,512]{1,0:T(8,128)(2,1)} %tsk_in.1, f32[512,256]{1,0:T(8,128)} %init.1), custom_call_target="tpu_custom_call" | custom-call | tf_op jit(solution)/shard_map/cca/pallas_call | solution.py:536
  152.2 1.9 %fusion = (bf16[640,256]{1,0:T(8,128)(2,1)}, bf16[640,256]{1,0:T(8,128)(2,1)}) fusion(bf16[640,512]{1,0:T(8,128)(2,1)} %get-tuple-element.6), kind=kLoop, calls=%fused_computation | loop fusion | bytes 1310720 | tf_op jit(solution)/shard_map/slice | solution.py:581
  154.1 1.3 slice.14
  155.4 1.6 slice.15

commit v6 on v5

--- a/solution.py
+++ b/solution.py
@@ -16,45 +16,42 @@
 
 def factor(d_ref):
     row = lax.broadcasted_iota(jnp.int32, (8, 128), 0)
+    lane = lax.broadcasted_iota(jnp.int32, (8, 128), 1)
     for p in range(16):
-        rows = slice(8 * p, 8 * p + 8)
-        gram, inverse = d_ref[rows, 0:128], d_ref[rows, 128:256]
+        lo, hi = 8 * p, 8 * p + 8
+        work = d_ref[lo:hi, 0:128]
         cell = {}
         for j in range(8):
-            column = jnp.broadcast_to(gram[:, 8 * p + j : 8 * p + j + 1], (8, 128))
-            for i in range(j, 8):
+            column = jnp.broadcast_to(work[:, lo + j : lo + j + 1], (8, 128))
+            for i in range(8):
                 cell[i, j] = column[i : i + 1, :]
-        scales = []
+        pivot = (lane >= lo) & (lane < hi)
+        work = jnp.where(pivot, jnp.where(lane - lo == row, 1.0, 0.0), work)
+        final = work
         for j in range(8):
-            scales.append(lax.rsqrt(cell[j, j]))
-            if j == 7:
-                break
-            inv = 1.0 / cell[j, j]
-            ratio = {i: cell[i, j] * inv for i in range(j + 1, 8)}
+            inv, root = 1.0 / cell[j, j], lax.rsqrt(cell[j, j])
+            here = work[j : j + 1, :]
+            final = jnp.where(row == j, jnp.broadcast_to(here * root, (8, 128)), final)
+            others = [i for i in range(8) if i != j]
+            ratio = {i: cell[i, j] * inv for i in others}
             for b in range(j + 1, 8):
-                for i in range(b, 8):
-                    cell[i, b] = cell[i, b] - ratio[i] * cell[b, j]
+                top = cell[j, b]
+                for i in others:
+                    cell[i, b] = cell[i, b] - ratio[i] * top
+                cell[j, b] = top * inv
             factors = jnp.zeros((8, 128), F32)
-            for i in range(j + 1, 8):
+            for i in others:
                 factors = jnp.where(row == i, jnp.broadcast_to(ratio[i], (8, 128)), factors)
-            inverse = inverse - factors * inverse[j : j + 1, :]
-            gram = gram - factors * gram[j : j + 1, :]
-        scale = jnp.broadcast_to(scales[0], (8, 128))
-        for i in range(1, 8):
-            scale = jnp.where(row == i, jnp.broadcast_to(scales[i], (8, 128)), scale)
-        upper, under = gram * scale, inverse * scale
-        d_ref[rows, 128:256] = under
-        if p < 15:
-            turned = upper.T
-            for g in range(p + 1, 16):
-                group = slice(8 * g, 8 * g + 8)
-                left, right = d_ref[group, 0:128], d_ref[group, 128:256]
-                for j in range(8):
-                    times = turned[group, j : j + 1]
-                    left = left - times * upper[j : j + 1, :]
-                    right = right - times * under[j : j + 1, :]
-                d_ref[group, 0:128] = left
-                d_ref[group, 128:256] = right
+            here = jnp.broadcast_to(here, (8, 128))
+            work = jnp.where(row == j, here * inv, work - factors * here)
+        d_ref[lo:hi, 128:256] = jnp.where(lane < hi, final, 0.0)
+        for g in range(p + 1, 16):
+            group = slice(8 * g, 8 * g + 8)
+            old = d_ref[group, 0:128]
+            new = jnp.where(pivot, 0.0, old)
+            for j in range(8):
+                new = new - old[:, lo + j : lo + j + 1] * work[j : j + 1, :]
+            d_ref[group, 0:128] = new
 
 
 MESH = pl.DeviceIdType.MESH
@@ -174,44 +171,55 @@
 
 def gram_stream(net, axes, source, land1, part1, land2, part2, land3, out3, out2, out1):
     place = net.place
-    first, second = axes
-    i1, i2, z = place.ring(first)[0], place.ring(second)[0], place.z
-    copies = net.scatter(first, lambda i: source.at[rows_of(i, 288)], land1)
-    yield
-    finish(copies)
-    part1[...] = source[rows_of(i1, 288)] + total_of(land1)
-    copies = net.scatter(second, lambda i: part1.at[rows_of(i, 72)], land2)
-    part2[72:128] = jnp.zeros((56, 128), F32)
-    yield
-    finish(copies)
-    part2[0:72] = part1[rows_of(i2, 72)] + total_of(land2)
-    copies = net.scatter("z", lambda i: part2.at[rows_of(i, 16)], land3)
-    yield
-    finish(copies)
-    out3[rows_of(z, 16)] = part2[rows_of(z, 16)] + total_of(land3)
-    copies = net.gather("z", out3.at[rows_of(z, 16)])
-    yield
-    finish(copies)
-    out2[i2] = out3[0:72]
-    copies = net.gather(second, out2.at[i2])
+    (i1, s1), (i2, s2), (i3, s3) = (place.ring(axis) for axis in axes)
+    r1, r2, r3 = part1.shape[0], land2.shape[1], land3.shape[1]
+    copies = net.scatter(axes[0], lambda i: source.at[rows_of(i, r1)], land1)
+    yield
+    finish(copies)
+    part1[...] = source[rows_of(i1, r1)] + total_of(land1)
+    copies = net.scatter(axes[1], lambda i: part1.at[rows_of(i, r2)], land2)
+    if r3 * s3 > r2:
+        part2[r2 : r3 * s3] = jnp.zeros((r3 * s3 - r2, 128), F32)
+    yield
+    finish(copies)
+    part2[0:r2] = part1[rows_of(i2, r2)] + total_of(land2)
+    copies = net.scatter(axes[2], lambda i: part2.at[rows_of(i, r3)], land3)
+    yield
+    finish(copies)
+    out3[rows_of(i3, r3)] = part2[rows_of(i3, r3)] + total_of(land3)
+    copies = net.gather(axes[2], out3.at[rows_of(i3, r3)])
+    yield
+    finish(copies)
+    out2[i2] = out3[0:r2]
+    copies = net.gather(axes[1], out2.at[i2])
     yield
     finish(copies)
     out1[i1] = out2[...]
-    copies = net.gather(first, out1.at[i1])
-    yield
-    finish(copies)
-
-
-GRAM_SCRATCH = [
-    pltpu.VMEM((3, 288, 128), F32),
-    pltpu.VMEM((288, 128), F32),
-    pltpu.VMEM((3, 72, 128), F32),
-    pltpu.VMEM((128, 128), F32),
-    pltpu.VMEM((7, 16, 128), F32),
-    pltpu.VMEM((128, 128), F32),
-    pltpu.VMEM((4, 72, 128), F32),
-    pltpu.VMEM((4, 4, 72, 128), F32),
-]
+    copies = net.gather(axes[0], out1.at[i1])
+    yield
+    finish(copies)
+
+
+GRAMS = (("xyz", 0, 1024), ("yxz", 1024, 1024), ("zxy", 2048, 256))
+
+
+def gram_scratch(axes, rows):
+    s1, s2, s3 = (8 if axis == "z" else 4 for axis in axes)
+    r1, r2 = rows // s1, rows // s1 // s2
+    r3 = -(-r2 // (8 * s3)) * 8
+    shapes = (
+        (s1 - 1, r1),
+        (r1,),
+        (s2 - 1, r2),
+        (r3 * s3,),
+        (s3 - 1, r3),
+        (r3 * s3,),
+        (s2, r2),
+        (s1, s2, r2),
+    )
+    return [pltpu.VMEM((*shape, 128), F32) for shape in shapes]
+
+
 UPPER = [(i, j) for j in range(4) for i in range(j + 1)]
 
 
@@ -333,7 +341,6 @@
             @pl.when(k == kk)
             def _():
                 d_ref[:, 0:128] = a_ref[128 * kk : 128 * kk + 128, 128 * kk : 128 * kk + 128]
-                d_ref[:, 128:256] = eye
 
         factor(d_ref)
         for kk in range(4):
@@ -357,10 +364,10 @@
 
 def cca_kernel(people, geno_in, freq, traits_in, gsk_in, tsk_in, init, scores, loads, *scratch):
     geno, traits, gsk, tsk, std, give, take, held, lands, both, source = scratch[:11]
-    alpha, beta = scratch[11:19], scratch[19:27]
-    a_ref, d_ref, inv, cross, full = scratch[27:32]
-    parts = [scratch[32 + 5 * s : 37 + 5 * s] for s in range(4)]
-    sends, recvs, loaded = scratch[52:55]
+    grams = [scratch[11 + 8 * s : 19 + 8 * s] for s in range(3)]
+    a_ref, d_ref, inv, cross, full = scratch[35:40]
+    parts = [scratch[40 + 5 * s : 45 + 5 * s] for s in range(4)]
+    sends, recvs, loaded = scratch[60:63]
     place = Place()
     net = Net(place, sends, recvs)
     x, k = place.x, place.core
@@ -444,15 +451,16 @@
             source[128 * t : 128 * t + 128] = crossed[128 * i : 128 * i + 128, 128 * j : 128 * j + 128]
     together(
         [
-            gram_stream(net, ("x", "y"), source.at[0:1152], *alpha),
-            gram_stream(net, ("y", "x"), source.at[1152:2304], *beta),
+            gram_stream(net, axes, source.at[first : first + rows], *buffers)
+            for (axes, first, rows), buffers in zip(GRAMS, grams)
         ]
     )
-    for s, stream in enumerate((alpha, beta)):
-        for i in range(4):
-            for j in range(4):
-                at = 1152 * s + 288 * i + 72 * j
-                source[at : at + 72] = stream[7][i, j]
+    for (_, first, rows), buffers in zip(GRAMS, grams):
+        s1, s2, r2 = buffers[7].shape[:3]
+        for i in range(s1):
+            for j in range(s2):
+                at = first + r2 * (s2 * i + j)
+                source[at : at + r2] = buffers[7][i, j]
 
     full[k * 4 + x] = both[k]
     full[(1 - k) * 4 + x] = both[1 - k]
@@ -532,7 +540,7 @@
 
 def cca(people, geno, freq, traits, gsk, tsk, init):
     vm, far = pl.BlockSpec(memory_space=pltpu.VMEM), pl.BlockSpec(memory_space=pl.ANY)
-    sems = 4 + 12 + 1 + 2 * (2 * (3 + 3 + 7)) + 3 + 1 + 4 + 3 + (6 + 14) + (6 + 7) + 2 * (14 + 3)
+    sems = 4 + 12 + 1 + 3 * (2 * (3 + 3 + 7)) + 3 + 1 + 4 + 3 + (6 + 14) + (6 + 7) + 2 * (14 + 3)
     return pl.pallas_call(
         functools.partial(cca_kernel, people),
         out_shape=[
@@ -553,8 +561,7 @@
             pltpu.VMEM((3, 4, 80, 256), F32),
             pltpu.VMEM((2, 80, 1024), F32),
             pltpu.VMEM((2304, 128), F32),
-            *GRAM_SCRATCH,
-            *GRAM_SCRATCH,
+            *[buffer for axes, _, rows in GRAMS for buffer in gram_scratch(axes, rows)],
             pltpu.VMEM((512, 1024), F32),
             pltpu.VMEM((128, 256), F32),
             pltpu.VMEM((2, 512, 512), F32),

time: 157 us -> 151 us (0.962)
  Pallas kernels: 152 us -> 145 us
    pallas_call x1, Pallas kernels: 152 us -> 145 us  [cca(): pl.pallas_call(functools.partial(cca_kernel, people), out_shape=[jax.Shap...]
where the time goes in v6:
time: 151 us; the launch traced here: 150 us
  Pallas kernels  145 us (96%)
  local copies, waits for them, and re-layouts  4.84 us (3%)
    pallas_call x1, Pallas kernels, cca(): pl.pallas_call(functools.partial(cca_kernel, people), out_shape=[jax.Shap...  145 us

profile of v6, /device:TPU:1, one launch (start us, length us, event | category | flops | bytes accessed | tf_op | source)
XLA Modules:
  0.0 150.3 jit_solution(3387240098347547278)
XLA Ops:
  0.6 144.8 %cca.1 = (bf16[640,512]{1,0:T(8,128)(2,1)}, f32[8,4608]{1,0:T(8,128)}) custom-call(s32[640,512]{1,0:T(8,128)} %geno_in.1, f32[1,512]{1,0:T(1,128)} %bitcast.1, bf16[640,4096]{1,0:T(8,128)(2,1)} %traits_in.1, bf16[512,512]{1,0:T(8,128)(2,1)} %gsk_in.1, bf16[4096,512]{1,0:T(8,128)(2,1)} %tsk_in.1, f32[512,256]{1,0:T(8,128)} %init.1), custom_call_target="tpu_custom_call" | custom-call | tf_op jit(solution)/shard_map/cca/pallas_call | solution.py:544
  145.5 1.9 %fusion = (bf16[640,256]{1,0:T(8,128)(2,1)}, bf16[640,256]{1,0:T(8,128)(2,1)}) fusion(bf16[640,512]{1,0:T(8,128)(2,1)} %get-tuple-element.6), kind=kLoop, calls=%fused_computation | loop fusion | bytes 1310720 | tf_op jit(solution)/shard_map/slice | solution.py:588
  147.4 1.3 slice.14
  148.7 1.6 %slice.15 = f32[8,4096]{1,0:T(8,128)} slice(f32[8,4608]{1,0:T(8,128)} %get-tuple-element.7), slice={[0:8], [512:4608]} | slice | bytes 262144 | tf_op jit(solution)/shard_map/slice | solution.py:588

commit v7 on v6

--- a/solution.py
+++ b/solution.py
@@ -237,7 +237,7 @@
 
 
 def unit(v):
-    return v * lax.rsqrt(jnp.mean(v * v, axis=0, keepdims=True) + 1e-06)
+    return v * lax.rsqrt(jnp.mean(v * v, axis=1, keepdims=True) + 1e-06)
 
 
 def rows_first(net, source, land1, part1, land2, out):
@@ -497,14 +497,14 @@
         pair.append(net.send(came, came, "core"))
     finish(swaps)
     pair[0].wait()
-    left = unit(dotf(inv[0], dotf(cross[...], dotf(inv[1], init[...], 0, 0), 1, 0), 1, 0))
+    left = unit(dotf(dotf(dotf(init[...].T, inv[1], 1, 0), cross[...], 1, 1), inv[0], 1, 1))
     scale = 1.0 / math.sqrt(inv.shape[1])
-    geno_weights = dotf(inv[0], left, 0, 0)
-    right = unit(dotf(inv[1], dotf(cross[...], geno_weights, 0, 0), 1, 0))
-    trait_weights = dotf(inv[1], right, 0, 0)
+    geno_weights = dotf(left, inv[0], 1, 0)
+    right = unit(dotf(dotf(geno_weights, cross[...], 1, 0), inv[1], 1, 1))
+    trait_weights = dotf(right, inv[1], 1, 0)
     finish(pair[1:])
     flat = full[...].reshape(640, 1024)
-    tscore = dotf(flat[:, 512:1024], trait_weights * scale, 1, 0).astype(jnp.bfloat16)
+    tscore = dotf(flat[:, 512:1024], trait_weights * scale, 1, 1).astype(jnp.bfloat16)
     trait_t = tscore.T
 
     def put(target, at, lhs, rhs):
@@ -523,7 +523,7 @@
             for at in range(0, count, 256):
                 put(target, at, trait_t, traits[:, first + at : first + at + 256])
             if genos:
-                gscore = dotf(flat[:, 0:512], geno_weights * scale, 1, 0).astype(jnp.bfloat16)
+                gscore = dotf(flat[:, 0:512], geno_weights * scale, 1, 1).astype(jnp.bfloat16)
                 scores[:, 0:256] = gscore
                 geno_t = gscore.T
             for at in range(0, genos, 256):

time: 151 us -> 145 us (0.960)
  Pallas kernels: 145 us -> 139 us
    pallas_call x1, Pallas kernels: 145 us -> 139 us  [cca(): pl.pallas_call(functools.partial(cca_kernel, people), out_shape=[jax.Shap...]
where the time goes in v7:
time: 145 us
  Pallas kernels  139 us (96%)
  local copies, waits for them, and re-layouts  4.84 us (3%)
    pallas_call x1, Pallas kernels, cca(): pl.pallas_call(functools.partial(cca_kernel, people), out_shape=[jax.Shap...  139 us

profile of v7, /device:TPU:1, one launch (start us, length us, event | category | flops | bytes accessed | tf_op | source)
XLA Modules:
  0.0 144.8 jit_solution(3123084672864585641)
XLA Ops:
  0.6 139.3 %cca.1 = (bf16[640,512]{1,0:T(8,128)(2,1)}, f32[8,4608]{1,0:T(8,128)}) custom-call(s32[640,512]{1,0:T(8,128)} %geno_in.1, f32[1,512]{1,0:T(1,128)} %bitcast.1, bf16[640,4096]{1,0:T(8,128)(2,1)} %traits_in.1, bf16[512,512]{1,0:T(8,128)(2,1)} %gsk_in.1, bf16[4096,512]{1,0:T(8,128)(2,1)} %tsk_in.1, f32[512,256]{1,0:T(8,128)} %init.1), custom_call_target="tpu_custom_call" | custom-call | tf_op jit(solution)/shard_map/cca/pallas_call | solution.py:544
  140.0 1.9 %fusion = (bf16[640,256]{1,0:T(8,128)(2,1)}, bf16[640,256]{1,0:T(8,128)(2,1)}) fusion(bf16[640,512]{1,0:T(8,128)(2,1)} %get-tuple-element.6), kind=kLoop, calls=%fused_computation | loop fusion | bytes 1310720 | tf_op jit(solution)/shard_map/slice | solution.py:588
  141.9 1.3 slice.14
  143.2 1.6 %slice.15 = f32[8,4096]{1,0:T(8,128)} slice(f32[8,4608]{1,0:T(8,128)} %get-tuple-element.7), slice={[0:8], [512:4608]} | slice | bytes 262144 | tf_op jit(solution)/shard_map/slice | solution.py:588
